TPU v7x, 1024 devices: a whole 4x8x16 slice. The times are simulated.
1024 devices in a mesh: dp: 32 (over x_lo, z), seq: 32 (over y, x_hi, core).
Axes of the slice: x: 4 (x_hi: 2, x_lo: 2; x = x_hi * 2 + x_lo), y: 8, z: 16, core: 2. Of those that a mesh axis runs over, the one named last changes fastest.
Arguments:
- tokens: bfloat16 [131072, 8192], P(('dp', 'seq')), may hold values from -6 to 6
- queries: bfloat16 [131072, 1024], P(('dp', 'seq')), may hold values from -110 to 110
- positions: int32 [131072], P(('dp', 'seq')), may hold values from 0 to 1023, as said below
- grad: float32 [8192, 256], P(('dp', 'seq')), may hold values from -6 to 6
- master: float32 [8192, 256], P(('dp', 'seq')), may hold values from -0.0625 to 0.0625
- moment1: float32 [8192, 256], P(('dp', 'seq')), may hold values from -1.8 to 1.8
- moment2: float32 [8192, 256], P(('dp', 'seq')), may hold values from 0.5 to 4
- step: int32 [1], replicated, may hold values from 1 to 8
Outputs:
- attention: bfloat16 [131072, 1024], P(('dp', 'seq'))
- new_master: float32 [8192, 256], P(('dp', 'seq'))
- new_first: float32 [8192, 256], P(('dp', 'seq'))
- new_second: float32 [8192, 256], P(('dp', 'seq'))
Inputs may be any that keep to these rules, and one draw needn't show every extreme that they name: `positions`: the sequence is a pack of documents of 1 to 1024 tokens, one of exactly 1024; a position is 0 at the first token of each document and rises by one from token to token inside a document.
All inputs are finite; a program needn't handle non-finite values.
Results may differ from a plain program's by a relative error of at most 0.014.
The roundings to bfloat16 on the way count: a program that leaves them out, or rounds other values in their place, can miss the bound.
Values may be sent and summed in bfloat16 or wider, within the bound.
No kernel may reach another device: no remote copies, remote signals or barrier semaphores. Data moves between devices by JAX's collectives and lax.ppermute only.
A program may use at most 32 MiB of HBM per device.

v0:
```python
import math

import jax
import jax.numpy as jnp
from jax import lax
from jax.experimental import pallas as pl
from jax.experimental.pallas import tpu as pltpu
from jax.sharding import Mesh
from jax.sharding import PartitionSpec as P


CORE = "core"
ALONG_Y = "y"
ALONG_Z = "z"
X_HI = "x_hi"
EVERY = ("x_lo", "z", "y", "x_hi", "core")
CHIPS = ("x_lo", "z", "y", "x_hi")


beta_one = 0.9
beta_two = 0.95
learn_rate = 0.02
adam_eps = 1e-08
rope_base = 500000.0
masked_score = -1e30


def adam_update(grad, master, moment1, moment2, step):
    counter = step[0].astype(jnp.float32)
    new_first = beta_one * moment1 + (1.0 - beta_one) * grad
    new_second = beta_two * moment2 + (1.0 - beta_two) * grad * grad
    fixed_first = new_first / (1.0 - jnp.power(jnp.float32(beta_one), counter))
    fixed_second = new_second / (1.0 - jnp.power(jnp.float32(beta_two), counter))
    new_master = master - learn_rate * fixed_first / (jnp.sqrt(fixed_second) + adam_eps)
    return (new_master, new_first, new_second)


def on_chip(count):
    return [pl.BlockSpec(memory_space=pltpu.VMEM)] * count


def room(mib):
    return pltpu.CompilerParams(vmem_limit_bytes=mib * 2**20)


def split_kernel(tokens_ref, out_ref):
    span = 512
    source = lax.broadcasted_iota(jnp.int32, (span, span), 0)
    target = lax.broadcasted_iota(jnp.int32, (span, span), 1)
    goal = (
        (((source >> 3) & 3) << 7)
        | ((source >> 8) << 6)
        | (((source >> 5) & 7) << 3)
        | (source & 7)
    )
    chosen = (goal == target).astype(jnp.float32).astype(jnp.bfloat16)
    count = tokens_ref.shape[0]
    for x_lo in range(2):
        stacked = jnp.concatenate(
            [
                tokens_ref[:, (8 * x_lo + part) * span : (8 * x_lo + part + 1) * span]
                for part in range(8)
            ],
            axis=0,
        )
        moved = jnp.dot(stacked, chosen, preferred_element_type=jnp.float32).astype(jnp.bfloat16)
        for part in range(8):
            for kind in range(4):
                out_ref[4 * x_lo + kind, :, part * 128 : (part + 1) * 128] = moved[
                    part * count : (part + 1) * count, kind * 128 : (kind + 1) * 128
                ]


def split_columns(tokens):
    count, width = tokens.shape
    return pl.pallas_call(
        split_kernel,
        out_shape=jax.ShapeDtypeStruct((8, count, width // 8), tokens.dtype),
        in_specs=on_chip(1),
        out_specs=on_chip(1)[0],
        compiler_params=room(20),
        cost_estimate=pl.CostEstimate(
            flops=2 * count * width * 512, bytes_accessed=4 * count * width, transcendentals=0
        ),
    )(tokens)


def partial_kernel(weight_ref, tokens_ref, out_ref):
    kinds, count, depth = tokens_ref.shape
    head_dim = weight_ref.shape[1] // 2
    part = jnp.dot(
        tokens_ref[...].reshape(kinds * count, depth),
        weight_ref[...],
        preferred_element_type=jnp.float32,
    )
    part = part.reshape(kinds, count, 2 * head_dim)
    keys = part[:, :, :head_dim]
    high = keys.astype(jnp.bfloat16)
    out_ref[:, :, :head_dim] = high
    out_ref[:, :, head_dim : 2 * head_dim] = (keys - high.astype(jnp.float32)).astype(jnp.bfloat16)
    out_ref[:, :, 2 * head_dim :] = part[:, :, head_dim:].astype(jnp.bfloat16)


def partial_products(weight, tokens):
    kinds, count, depth = tokens.shape
    width = weight.shape[1] // 2 * 3
    return pl.pallas_call(
        partial_kernel,
        out_shape=jax.ShapeDtypeStruct((kinds, count, width), jnp.bfloat16),
        in_specs=on_chip(2),
        out_specs=on_chip(1)[0],
        compiler_params=room(20),
        cost_estimate=pl.CostEstimate(
            flops=2 * kinds * count * weight.shape[1] * depth,
            bytes_accessed=2 * kinds * count * (width + depth),
            transcendentals=0,
        ),
    )(weight, tokens)


def turned(values, cosine, sine):
    return values * cosine + pltpu.roll(values, values.shape[1] // 2, 1) * sine


def sum_kernel(parts_ref, cosine_ref, sine_ref, out_ref):
    head_dim = parts_ref.shape[2] // 3
    total = jnp.sum(parts_ref[...].astype(jnp.float32), axis=0)
    keys = total[:, :head_dim] + total[:, head_dim : 2 * head_dim]
    out_ref[:, :head_dim] = turned(keys, cosine_ref[...], sine_ref[...]).astype(jnp.bfloat16)
    out_ref[:, head_dim:] = total[:, 2 * head_dim :].astype(jnp.bfloat16)


def summed(parts, cosine, sine):
    kinds, count, width = parts.shape
    return pl.pallas_call(
        sum_kernel,
        out_shape=jax.ShapeDtypeStruct((count, width // 3 * 2), jnp.bfloat16),
        in_specs=on_chip(3),
        out_specs=on_chip(1)[0],
        compiler_params=room(8),
        cost_estimate=pl.CostEstimate(
            flops=kinds * count * width, bytes_accessed=2 * kinds * count * width, transcendentals=0
        ),
    )(parts, cosine, sine)


def attend_kernel(
    offset_ref, back_ref, row_ref, queries_ref, first_ref, cosine_ref, sine_ref, out_ref, window
):
    count, width = queries_ref.shape
    head_dim = cosine_ref.shape[1]
    held, reach = back_ref.shape[0], window.shape[0] - row_ref.shape[0]
    window[:held] = back_ref[...]
    window[held:] = row_ref[...]
    seen = reach + count
    near = pl.ds(pl.multiple_of(offset_ref[0], 128), seen)
    keys = window[near, :head_dim]
    values = window[near, head_dim:]
    row = lax.broadcasted_iota(jnp.int32, (count, head_dim), 0)
    column = lax.broadcasted_iota(jnp.int32, (count, head_dim), 1)
    first = first_ref[...]
    bias = jnp.concatenate(
        [
            jnp.where(
                (column + (start - reach) <= row) & (column + (start - reach) >= first),
                0.0,
                masked_score,
            )
            for start in range(0, seen, head_dim)
        ],
        axis=1,
    )
    cosine, sine = cosine_ref[...], sine_ref[...]
    scale = head_dim**-0.5 * math.log2(math.e)
    for head in range(width // head_dim):
        lanes = slice(head * head_dim, (head + 1) * head_dim)
        rows = turned(queries_ref[:, lanes].astype(jnp.float32), cosine, sine)
        scores = lax.dot_general(
            rows.astype(jnp.bfloat16),
            keys,
            (((1,), (1,)), ((), ())),
            preferred_element_type=jnp.float32,
        )
        scores = scores + bias
        top_score = jnp.max(scores, axis=1, keepdims=True)
        weights = jnp.exp2((scores - top_score) * scale)
        share = 1.0 / jnp.sum(weights, axis=1, keepdims=True)
        probs = (weights * share).astype(jnp.bfloat16)
        out_ref[:, lanes] = jnp.dot(
            probs, values, preferred_element_type=jnp.float32
        ).astype(jnp.bfloat16)


def attend(offset, back, row, queries, first, cosine, sine):
    count, width = queries.shape
    return pl.pallas_call(
        attend_kernel,
        out_shape=jax.ShapeDtypeStruct((count, width), jnp.bfloat16),
        in_specs=[pl.BlockSpec(memory_space=pltpu.SMEM), *on_chip(6)],
        out_specs=on_chip(1)[0],
        scratch_shapes=[pltpu.VMEM((back.shape[0] + row.shape[0], row.shape[1]), jnp.bfloat16)],
        compiler_params=room(20),
        cost_estimate=pl.CostEstimate(
            flops=4 * count * width * 1152,
            bytes_accessed=4 * count * width + 2 * back.size + 2 * row.size,
            transcendentals=count * width * 9,
        ),
    )(offset, back, row, queries, first, cosine, sine)


def rotation_tables(places, head_dim):
    half_width = head_dim // 2
    freqs = jnp.exp(
        jnp.arange(half_width, dtype=jnp.float32) * (-2.0 * math.log(rope_base) / head_dim)
    )
    angles = places.astype(jnp.float32)[:, None] * freqs
    cosine = jnp.cos(angles)
    sine = jnp.sin(angles)
    return (
        jnp.concatenate([cosine, cosine], axis=1),
        jnp.concatenate([-sine, sine], axis=1),
    )


def shifted(value, axis, steps):
    count = lax.axis_size(axis)
    return lax.ppermute(value, axis, [(source, source + steps) for source in range(count - steps)])


def compute(tokens, queries, positions, grad, master, moment1, moment2, step):
    head_dim = master.shape[1] // 2
    local_count = tokens.shape[0]
    ring = ("x_lo", "x_hi", "core")
    new_master, new_first, new_second = adam_update(grad, master, moment1, moment2, step)
    weight = new_master.astype(jnp.bfloat16)
    over_z = lax.all_gather(weight, ALONG_Z, axis=0, tiled=True)
    sorted_tokens = split_columns(tokens)
    tokens_here = lax.all_to_all(
        sorted_tokens, ring, split_axis=0, concat_axis=0, tiled=True
    )
    cosine, sine = rotation_tables(positions, head_dim)
    first = jnp.broadcast_to(
        (jnp.arange(local_count, dtype=jnp.int32) - positions)[:, None],
        (local_count, head_dim),
    )
    over_y = lax.all_gather(over_z, ALONG_Y, axis=0, tiled=True)
    size = lax.axis_size
    rows_here = over_y.reshape(size(ALONG_Y), size(ALONG_Z), weight.shape[0], 2 * head_dim)
    rows_here = rows_here.transpose(1, 0, 2, 3).reshape(-1, 2 * head_dim)
    parts = partial_products(rows_here, tokens_here)
    parts = lax.all_to_all(parts, ring, split_axis=0, concat_axis=0, tiled=True)
    key_value = summed(parts, cosine, sine)
    row_kv = lax.all_gather(key_value, X_HI, axis=0)
    one_back = shifted(row_kv, CHIPS, 2)
    two_back = shifted(row_kv, CHIPS, 4)
    row_both = lax.all_gather(row_kv, CORE, axis=1)
    back_both = lax.all_gather(jnp.concatenate([two_back, one_back], axis=0), CORE, axis=1)
    offset = lax.axis_index(("x_hi", "core")) * local_count
    attention = attend(
        offset.astype(jnp.int32)[None],
        back_both.reshape(-1, 2 * head_dim),
        row_both.reshape(-1, 2 * head_dim),
        queries,
        first,
        cosine,
        sine,
    )
    return (attention, new_master, new_first, new_second)


def solution(mesh):
    finer = Mesh(mesh.devices.reshape(2, 16, 8, 2, 2), EVERY)
    rows = P(EVERY, None)
    placed = (rows, rows, P(EVERY), rows, rows, rows, rows, P())
    return jax.shard_map(
        compute,
        mesh=finer,
        in_specs=placed,
        out_specs=(rows, rows, rows, rows),
        check_vma=False,
    )
```

profile of v0, /device:TPU:6, one launch (start us, length us, event | category | flops | bytes accessed | tf_op | source)
XLA Modules:
  0.0 128.4 jit_solution(16670821595727314705)
XLA Ops:
  0.6 0.0 copy-start.1
  0.6 1.6 %copy-done.1 = bf16[128,8192]{1,0:T(8,128)(2,1)S(1)} copy-done((bf16[128,8192]{1,0:T(8,128)(2,1)S(1)}, bf16[128,8192]{1,0:T(8,128)(2,1)}, u32[]{:S(2)}) %copy-start.1) | copy-done | bytes 2097176
  2.2 1.5 %shard_map.111 = bf16[8,128,1024]{2,1,0:T(8,128)(2,1)S(1)} custom-call(bf16[128,8192]{1,0:T(8,128)(2,1)S(1)} %copy-done.1), custom_call_target="tpu_custom_call" | custom-call | flops 1073741824 | bytes 4194304 | tf_op jit(solution)/shard_map/pallas_call | solution.py:76
  3.7 0.0 copy-start
  3.7 1.3 %copy-done = bf16[8,128,1024]{2,1,0:T(8,128)(2,1)} copy-done((bf16[8,128,1024]{2,1,0:T(8,128)(2,1)}, bf16[8,128,1024]{2,1,0:T(8,128)(2,1)S(1)}, u32[]{:S(2)}) %copy-start) | copy-done | bytes 2097176
  5.1 0.0 copy-start.3
  5.1 0.0 copy-start.4
  5.1 0.0 copy-start.5
  5.1 0.0 copy-start.6
  5.1 16.8 %all-to-all-start = ((bf16[8,128,1024]{2,1,0:T(8,128)(2,1)}), bf16[8,128,1024]{2,1,0:T(8,128)(2,1)S(1)}, u32[]{:S(2)}, u32[]{:S(2)}) async-start(bf16[8,128,1024]{2,1,0:T(8,128)(2,1)} %copy-done), calls=%async_computation | async-start | bytes 4194304 | tf_op jit(solution)/shard_map/all_to_all | solution.py:238
  22.6 0.0 copy-done.3
  22.6 0.0 copy-done.4
  22.6 0.0 copy-done.5
  22.6 0.0 copy-done.6
  22.6 0.6 fusion.2
  23.3 30.7 %all_gather.24 = bf16[128,256]{1,0:T(8,128)(2,1)S(1)} all-gather(bf16[8,256]{1,0:T(8,128)(2,1)S(1)} %get-tuple-element.4), channel_id=1, replica_groups=mesh['x_lo'=2,'z'=16,'y'=8,'x_hi'=2,'core'=2] {'z'}, dimensions={0}, use_global_device_ids=true | all-gather | bytes 69632 | tf_op jit(solution)/shard_map/all_gather | solution.py:236
  53.9 26.8 %all_gather.25 = bf16[1024,256]{1,0:T(8,128)(2,1)S(1)} all-gather(bf16[128,256]{1,0:T(8,128)(2,1)S(1)} %all_gather.24), channel_id=1, replica_groups=mesh['x_lo'=2,'z'=16,'y'=8,'x_hi'=2,'core'=2] {'y'}, dimensions={0}, use_global_device_ids=true | all-gather | bytes 589824 | tf_op jit(solution)/shard_map/all_gather | solution.py:246
  80.8 0.0 all-to-all-done.tokens_ref
  80.8 0.0 copy-start.7
  80.9 1.6 %shard_map.112 = bf16[8,128,384]{2,1,0:T(8,128)(2,1)} custom-call(bf16[1024,256]{1,0:T(8,128)(2,1)S(1)} %bitcast.10, bf16[8,128,1024]{2,1,0:T(8,128)(2,1)S(1)} %all-to-all-done.tokens_ref), custom_call_target="tpu_custom_call" | custom-call | flops 536870912 | bytes 2883584 | tf_op jit(solution)/shard_map/pallas_call | solution.py:107
  82.5 5.0 %all-to-all-start.1 = ((bf16[8,128,384]{2,1,0:T(8,128)(2,1)}), bf16[8,128,384]{2,1,0:T(8,128)(2,1)S(1)}, u32[]{:S(2)}, u32[]{:S(2)}) async-start(bf16[8,128,384]{2,1,0:T(8,128)(2,1)} %shard_map.112), calls=%async_computation.1 | async-start | bytes 1572864 | tf_op jit(solution)/shard_map/all_to_all | solution.py:251
  87.5 0.0 copy-start.2
  87.5 0.0 copy-done.7
  87.5 0.3 fusion
  87.8 0.1 pad_maximum_fusion.1
  88.0 10.0 %all-to-all-done.1.parts_ref = bf16[8,128,384]{2,1,0:T(8,128)(2,1)S(1)} async-done(((bf16[8,128,384]{2,1,0:T(8,128)(2,1)}), bf16[8,128,384]{2,1,0:T(8,128)(2,1)S(1)}, u32[]{:S(2)}, u32[]{:S(2)}) %all-to-all-start.1) | async-done | bytes 786464 | tf_op jit(solution)/shard_map/all_to_all | solution.py:251
  98.0 0.1 shard_map.113
  98.1 6.4 %all-gather = bf16[256,256]{1,0:T(8,128)(2,1)S(1)} all-gather(bf16[128,256]{1,0:T(8,128)(2,1)S(1)} %shard_map.113), channel_id=2, replica_groups=mesh['x_lo'=2,'z'=16,'y'=8,'x_hi'=2,'core'=2] {'x_hi'}, dimensions={0}, use_global_device_ids=true | all-gather | bytes 196608 | tf_op jit(solution)/shard_map/all_gather | solution.py:253
  104.6 2.6 %collective-permute-start.1 = (bf16[2,128,256]{2,1,0:T(8,128)(2,1)S(1)}, bf16[2,128,256]{2,1,0:T(8,128)(2,1)S(1)}, u32[]{:S(2)}, u32[]{:S(2)}) collective-permute-start(bf16[2,128,256]{2,1,0:T(8,128)(2,1)S(1)} %bitcast.14), channel_id=1, source_target_pairs={{0,4},{2,6},{4,8},{6,10},{8,12},{10,14},{12,16},{14,18},{16,20},{1... | collective-permute-start | bytes 393224 | tf_op jit(solution)/shard_map/ppermute | solution.py:227
  107.2 4.1 %collective-permute-start = (bf16[2,128,256]{2,1,0:T(8,128)(2,1)S(1)}, bf16[2,128,256]{2,1,0:T(8,128)(2,1)S(1)}, u32[]{:S(2)}, u32[]{:S(2)}) collective-permute-start(bf16[2,128,256]{2,1,0:T(8,128)(2,1)S(1)} %bitcast.15), channel_id=1, source_target_pairs={{0,8},{2,10},{4,12},{6,14},{8,16},{10,18},{12,20},{14,22},{16,24},... | collective-permute-start | bytes 393224 | tf_op jit(solution)/shard_map/ppermute | solution.py:227
  111.3 2.0 %all-gather.2 = bf16[2,256,256]{2,1,0:T(8,128)(2,1)S(1)} all-gather(bf16[2,128,256]{2,1,0:T(8,128)(2,1)S(1)} %bitcast.16), channel_id=4, replica_groups=mesh['x_lo'=2,'z'=16,'y'=8,'x_hi'=2,'core'=2] {'core'}, dimensions={1}, use_global_device_ids=true | all-gather | bytes 393216 | tf_op jit(solution)/shard_map/all_gather | solution.py:256
  113.3 3.6 %collective-permute-done.1 = bf16[2,128,256]{2,1,0:T(8,128)(2,1)S(1)} collective-permute-done((bf16[2,128,256]{2,1,0:T(8,128)(2,1)S(1)}, bf16[2,128,256]{2,1,0:T(8,128)(2,1)S(1)}, u32[]{:S(2)}, u32[]{:S(2)}) %collective-permute-start.1) | collective-permute-done | bytes 131104 | tf_op jit(solution)/shard_map/ppermute | solution.py:227
  116.9 4.3 %collective-permute-done = bf16[2,128,256]{2,1,0:T(8,128)(2,1)S(1)} collective-permute-done((bf16[2,128,256]{2,1,0:T(8,128)(2,1)S(1)}, bf16[2,128,256]{2,1,0:T(8,128)(2,1)S(1)}, u32[]{:S(2)}, u32[]{:S(2)}) %collective-permute-start) | collective-permute-done | bytes 131104 | tf_op jit(solution)/shard_map/ppermute | solution.py:227
  121.3 2.2 %all-gather.1 = bf16[4,256,256]{2,1,0:T(8,128)(2,1)S(1)} all-gather(bf16[4,128,256]{2,1,0:T(8,128)(2,1)S(1)} %pad_maximum_fusion), channel_id=3, replica_groups=mesh['x_lo'=2,'z'=16,'y'=8,'x_hi'=2,'core'=2] {'core'}, dimensions={1}, use_global_device_ids=true | all-gather | bytes 786432 | tf_op jit(solution)/shard_map/all_gather | solution.py:257
  123.5 0.1 broadcast_in_dim.5.first_ref
  123.5 0.0 copy-done.2
  123.6 4.9 %shard_map.114 = bf16[128,1024]{1,0:T(8,128)(2,1)} custom-call(s32[1]{0:T(128)} %bitcast.offset_ref, bf16[1024,256]{1,0:T(8,128)(2,1)S(1)} %bitcast.11, bf16[512,256]{1,0:T(8,128)(2,1)S(1)} %bitcast.12, bf16[128,1024]{1,0:T(8,128)(2,1)S(1)} %copy-done.2, s32[128,128]{1,0:T(8,128)S(1)} %broadcast_in_dim.5.first_ref, ...), custom_call_target="tpu_custom_call" | custom-call | flops 603979776 | bytes 1310720 | tf_op jit(solution)/shard_map/pallas_call | solution.py:196
  (4 shorter events, 0.1 us)
Async XLA Ops:
  0.6 1.6 %copy-start.1 = (bf16[128,8192]{1,0:T(8,128)(2,1)S(1)}, bf16[128,8192]{1,0:T(8,128)(2,1)}, u32[]{:S(2)}) copy-start(bf16[128,8192]{1,0:T(8,128)(2,1)} %tokens_ref.1) | copy-start | bytes 6291460
  3.7 1.3 %copy-start = (bf16[8,128,1024]{2,1,0:T(8,128)(2,1)}, bf16[8,128,1024]{2,1,0:T(8,128)(2,1)S(1)}, u32[]{:S(2)}) copy-start(bf16[8,128,1024]{2,1,0:T(8,128)(2,1)S(1)} %shard_map.111) | copy-start | bytes 6291460
  5.1 17.5 %copy-start.3 = (f32[8,256]{1,0:T(8,128)S(1)}, f32[8,256]{1,0:T(8,128)}, u32[]{:S(2)}) copy-start(f32[8,256]{1,0:T(8,128)} %param.12) | copy-start | bytes 24580
  5.1 17.5 %copy-start.4 = (f32[8,256]{1,0:T(8,128)S(1)}, f32[8,256]{1,0:T(8,128)}, u32[]{:S(2)}) copy-start(f32[8,256]{1,0:T(8,128)} %param.11) | copy-start | bytes 24580
  5.1 17.5 %copy-start.5 = (f32[8,256]{1,0:T(8,128)S(1)}, f32[8,256]{1,0:T(8,128)}, u32[]{:S(2)}) copy-start(f32[8,256]{1,0:T(8,128)} %param.13) | copy-start | bytes 24580
  5.1 17.6 %copy-start.6 = (f32[8,256]{1,0:T(8,128)S(1)}, f32[8,256]{1,0:T(8,128)}, u32[]{:S(2)}) copy-start(f32[8,256]{1,0:T(8,128)} %param.14) | copy-start | bytes 24580
  5.1 75.8 %all-to-all-start = ((bf16[8,128,1024]{2,1,0:T(8,128)(2,1)}), bf16[8,128,1024]{2,1,0:T(8,128)(2,1)S(1)}, u32[]{:S(2)}, u32[]{:S(2)}) async-start(bf16[8,128,1024]{2,1,0:T(8,128)(2,1)} %copy-done), calls=%async_computation | async-start | bytes 4194304 | tf_op jit(solution)/shard_map/all_to_all | solution.py:238
  80.8 6.7 %copy-start.7 = (s32[128]{0:T(128)S(1)}, s32[128]{0:T(128)}, u32[]{:S(2)}) copy-start(s32[128]{0:T(128)} %param.10) | copy-start | bytes 1540
  82.5 15.5 %all-to-all-start.1 = ((bf16[8,128,384]{2,1,0:T(8,128)(2,1)}), bf16[8,128,384]{2,1,0:T(8,128)(2,1)S(1)}, u32[]{:S(2)}, u32[]{:S(2)}) async-start(bf16[8,128,384]{2,1,0:T(8,128)(2,1)} %shard_map.112), calls=%async_computation.1 | async-start | bytes 1572864 | tf_op jit(solution)/shard_map/all_to_all | solution.py:251
  87.5 36.0 %copy-start.2 = (bf16[128,1024]{1,0:T(8,128)(2,1)S(1)}, bf16[128,1024]{1,0:T(8,128)(2,1)}, u32[]{:S(2)}) copy-start(bf16[128,1024]{1,0:T(8,128)(2,1)} %queries_ref.1) | copy-start | bytes 786436
  104.6 12.4 %collective-permute-start.1 = (bf16[2,128,256]{2,1,0:T(8,128)(2,1)S(1)}, bf16[2,128,256]{2,1,0:T(8,128)(2,1)S(1)}, u32[]{:S(2)}, u32[]{:S(2)}) collective-permute-start(bf16[2,128,256]{2,1,0:T(8,128)(2,1)S(1)} %bitcast.14), channel_id=1, source_target_pairs={{0,4},{2,6},{4,8},{6,10},{8,12},{10,14},{12,16},{14,18},{16,20},{1... | collective-permute-start | bytes 393224 | tf_op jit(solution)/shard_map/ppermute | solution.py:227
  107.2 14.1 %collective-permute-start = (bf16[2,128,256]{2,1,0:T(8,128)(2,1)S(1)}, bf16[2,128,256]{2,1,0:T(8,128)(2,1)S(1)}, u32[]{:S(2)}, u32[]{:S(2)}) collective-permute-start(bf16[2,128,256]{2,1,0:T(8,128)(2,1)S(1)} %bitcast.15), channel_id=1, source_target_pairs={{0,8},{2,10},{4,12},{6,14},{8,16},{10,18},{12,20},{14,22},{16,24},... | collective-permute-start | bytes 393224 | tf_op jit(solution)/shard_map/ppermute | solution.py:227
where the time goes:
time: 130 us; the launch traced here: 128 us
  blocking collectives  68.1 us (52%)
  starting transfers between devices  28.5 us (22%)
  waiting for transfers between devices  18 us (14%)
  Pallas kernels  8.1 us (6%)
  local copies, waits for them, and re-layouts  3.06 us (2%)
  between operations  1.52 us (1%)
    all_gather x1, blocking collectives, compute(): over_z = lax.all_gather(weight, ALONG_Z, axis=0, tiled=True)  30.7 us
    all_gather x1, blocking collectives, compute(): over_y = lax.all_gather(over_z, ALONG_Y, axis=0, tiled=True)  26.8 us
    all_to_all x1, starting transfers between devices, compute(): lax.all_to_all(sorted_tokens, ring, split_axis=0, concat_axis=0, tiled=True)  16.8 us
    all_to_all x1, waiting for transfers between devices, compute(): parts = lax.all_to_all(parts, ring, split_axis=0, concat_axis=0, tiled=True)  10 us
    ppermute x2, waiting for transfers between devices, shifted(): lax.ppermute(value, axis, [(source, source + steps) for source in range(c...  7.94 us
    ppermute x2, starting transfers between devices, shifted(): lax.ppermute(value, axis, [(source, source + steps) for source in range(c...  6.73 us
    all_gather x1, blocking collectives, compute(): row_kv = lax.all_gather(key_value, X_HI, axis=0)  6.44 us
    all_to_all x1, starting transfers between devices, compute(): parts = lax.all_to_all(parts, ring, split_axis=0, concat_axis=0, tiled=True)  5.03 us
  transfers between devices with their start and end apart: 4, of which 3 were waited for; matrix products, arithmetic and copies ran while one was open for 1% of the time, Pallas kernels for 0%

commit v1 on v0

v1 whole, which is shorter than its diff:
```python
import math

import jax
import jax.numpy as jnp
from jax import lax
from jax.experimental import pallas as pl
from jax.experimental.pallas import tpu as pltpu
from jax.sharding import Mesh
from jax.sharding import PartitionSpec as P


CORE = "core"
ALONG_X = ("x_lo", "x_hi")
ALONG_Y = "y"
ALONG_Z = "z"
X_HI = "x_hi"
EVERY = ("x_lo", "z", "y", "x_hi", "core")
CHIPS = ("x_lo", "z", "y", "x_hi")


beta_one = 0.9
beta_two = 0.95
learn_rate = 0.02
adam_eps = 1e-08
rope_base = 500000.0
masked_score = -1e30


def from_everyone(x, axis):
    copies = jnp.broadcast_to(x, (lax.axis_size(axis), *x.shape))
    return lax.all_to_all(copies, axis, split_axis=0, concat_axis=0, tiled=True)


def adam_update(grad, master, moment1, moment2, step):
    counter = step[0].astype(jnp.float32)
    new_first = beta_one * moment1 + (1.0 - beta_one) * grad
    new_second = beta_two * moment2 + (1.0 - beta_two) * grad * grad
    fixed_first = new_first / (1.0 - jnp.power(jnp.float32(beta_one), counter))
    fixed_second = new_second / (1.0 - jnp.power(jnp.float32(beta_two), counter))
    new_master = master - learn_rate * fixed_first / (jnp.sqrt(fixed_second) + adam_eps)
    return (new_master, new_first, new_second)


def on_chip(count):
    return [pl.BlockSpec(memory_space=pltpu.VMEM)] * count


def room(mib):
    return pltpu.CompilerParams(vmem_limit_bytes=mib * 2**20)


def split_kernel(tokens_ref, out_ref):
    span = 256
    source = lax.broadcasted_iota(jnp.int32, (span, span), 0)
    target = lax.broadcasted_iota(jnp.int32, (span, span), 1)
    goal = (((source >> 4) & 1) << 7) | ((source >> 5) << 4) | (source & 15)
    chosen = (goal == target).astype(jnp.float32).astype(jnp.bfloat16)
    count = tokens_ref.shape[0]
    for x_lo in range(2):
        for eight in range(2):
            first = (2 * x_lo + eight) * 8
            stacked = jnp.concatenate(
                [tokens_ref[:, part * span : (part + 1) * span] for part in range(first, first + 8)],
                axis=0,
            )
            moved = jnp.dot(stacked, chosen, preferred_element_type=jnp.float32)
            moved = moved.astype(jnp.bfloat16)
            for part in range(8):
                place = slice((8 * eight + part) * 128, (8 * eight + part + 1) * 128)
                for x_hi in range(2):
                    out_ref[x_lo + 2 * x_hi, :, place] = moved[
                        part * count : (part + 1) * count, x_hi * 128 : (x_hi + 1) * 128
                    ]


def split_columns(tokens):
    count, width = tokens.shape
    return pl.pallas_call(
        split_kernel,
        out_shape=jax.ShapeDtypeStruct((4, count, width // 4), tokens.dtype),
        in_specs=on_chip(1),
        out_specs=on_chip(1)[0],
        compiler_params=room(20),
        cost_estimate=pl.CostEstimate(
            flops=2 * count * width * 256, bytes_accessed=4 * count * width, transcendentals=0
        ),
    )(tokens)


def plane_product(mine_ref, theirs_ref, plane, halves, columns):
    depth = 16
    for half, half_ref in enumerate(halves):
        for y in range(4):
            for z in range(16):
                place = (z * 8 + 4 * half + y) * depth
                columns[place : place + depth] = half_ref[
                    (y * 16 + z) * depth : (y * 16 + z + 1) * depth
                ]
    rows = jnp.concatenate([mine_ref[plane], theirs_ref[plane]], axis=0)
    return jnp.dot(rows, columns[...], preferred_element_type=jnp.float32)


def own_kernel(place_ref, mine_ref, theirs_ref, low_ref, high_ref, out_ref, columns):
    out_ref[...] = plane_product(
        mine_ref, theirs_ref, place_ref[1], (low_ref, high_ref), columns
    )


def beside_kernel(
    place_ref, so_far_ref, mine_ref, theirs_ref, *pieces_and_out
):
    left_low, left_high, right_low, right_high, out_ref, columns, more = pieces_and_out
    left = (place_ref[1] + 3) & 3
    right = (place_ref[1] + 1) & 3
    out_ref[...] = (
        so_far_ref[...]
        + plane_product(mine_ref, theirs_ref, left, (left_low, left_high), columns)
        + plane_product(mine_ref, theirs_ref, right, (right_low, right_high), more)
    )


def across_kernel(
    place_ref, so_far_ref, mine_ref, theirs_ref, low_ref, high_ref, cosine_ref, sine_ref,
    out_ref, columns,
):
    across = (place_ref[1] + 2) & 3
    core = place_ref[0]
    total = so_far_ref[...] + plane_product(
        mine_ref, theirs_ref, across, (low_ref, high_ref), columns
    )
    count = mine_ref.shape[1]
    done = turned(total, cosine_ref[...], sine_ref[...]).astype(jnp.bfloat16)
    out_ref[pl.ds(pl.multiple_of(core * count, count), count)] = done[:count]
    out_ref[pl.ds(pl.multiple_of((1 - core) * count, count), count)] = done[count:]


def product(kernel, place, tiles, dtype, scratches, *operands):
    rows, width = tiles
    return pl.pallas_call(
        kernel,
        out_shape=jax.ShapeDtypeStruct(tiles, dtype),
        in_specs=[pl.BlockSpec(memory_space=pltpu.SMEM), *on_chip(len(operands))],
        out_specs=on_chip(1)[0],
        scratch_shapes=[pltpu.VMEM((2048, width), jnp.bfloat16)] * scratches,
        compiler_params=room(8),
        cost_estimate=pl.CostEstimate(
            flops=2 * rows * width * 2048 * scratches,
            bytes_accessed=2 * 2048 * (rows + width) * scratches,
            transcendentals=0,
        ),
    )(place, *operands)


def turned(values, cosine, sine):
    return values * cosine + pltpu.roll(values, values.shape[1] // 2, 1) * sine


def attend_kernel(
    offset_ref, back_ref, row_ref, queries_ref, first_ref, cosine_ref, sine_ref, out_ref, *windows
):
    count, width = queries_ref.shape
    head_dim = cosine_ref.shape[1]
    reach = back_ref.shape[1]
    seen = reach + count
    near = pl.ds(pl.multiple_of(offset_ref[0], 128), seen)
    for kind, window in enumerate(windows):
        window[:reach] = back_ref[kind]
        window[reach:] = row_ref[kind]
    keys, values = (window[near] for window in windows)
    row = lax.broadcasted_iota(jnp.int32, (count, head_dim), 0)
    column = lax.broadcasted_iota(jnp.int32, (count, head_dim), 1)
    first = first_ref[...]
    bias = jnp.concatenate(
        [
            jnp.where(
                (column + (start - reach) <= row) & (column + (start - reach) >= first),
                0.0,
                masked_score,
            )
            for start in range(0, seen, head_dim)
        ],
        axis=1,
    )
    cosine, sine = cosine_ref[...], sine_ref[...]
    scale = head_dim**-0.5 * math.log2(math.e)
    for head in range(width // head_dim):
        lanes = slice(head * head_dim, (head + 1) * head_dim)
        rows = turned(queries_ref[:, lanes].astype(jnp.float32), cosine, sine)
        scores = lax.dot_general(
            rows.astype(jnp.bfloat16),
            keys,
            (((1,), (1,)), ((), ())),
            preferred_element_type=jnp.float32,
        )
        scores = scores + bias
        top_score = jnp.max(scores, axis=1, keepdims=True)
        weights = jnp.exp2((scores - top_score) * scale)
        share = 1.0 / jnp.sum(weights, axis=1, keepdims=True)
        probs = (weights * share).astype(jnp.bfloat16)
        out_ref[:, lanes] = jnp.dot(
            probs, values, preferred_element_type=jnp.float32
        ).astype(jnp.bfloat16)


def attend(offset, back, row, queries, first, cosine, sine):
    count, width = queries.shape
    return pl.pallas_call(
        attend_kernel,
        out_shape=jax.ShapeDtypeStruct((count, width), jnp.bfloat16),
        in_specs=[pl.BlockSpec(memory_space=pltpu.SMEM), *on_chip(6)],
        out_specs=on_chip(1)[0],
        scratch_shapes=[pltpu.VMEM((back.shape[1] + row.shape[1], row.shape[2]), jnp.bfloat16)] * 2,
        compiler_params=room(20),
        cost_estimate=pl.CostEstimate(
            flops=4 * count * width * 1152,
            bytes_accessed=4 * count * width + 2 * back.size + 2 * row.size,
            transcendentals=count * width * 9,
        ),
    )(offset, back, row, queries, first, cosine, sine)


def rotation_tables(places, head_dim):
    half_width = head_dim // 2
    freqs = jnp.exp(
        jnp.arange(half_width, dtype=jnp.float32) * (-2.0 * math.log(rope_base) / head_dim)
    )
    angles = places.astype(jnp.float32)[:, None] * freqs
    cosine = jnp.cos(angles)
    sine = jnp.sin(angles)
    return (
        jnp.concatenate([cosine, cosine], axis=1),
        jnp.concatenate([-sine, sine], axis=1),
    )


def shifted(value, axis, steps):
    count = lax.axis_size(axis)
    return lax.ppermute(value, axis, [(source, source + steps) for source in range(count - steps)])


def along_x(value, steps):
    pairs = []
    for x_lo in range(2):
        for x_hi in range(2):
            goal = (2 * x_hi + x_lo + steps) % 4
            pairs.append((2 * x_lo + x_hi, 2 * (goal % 2) + goal // 2))
    return lax.ppermute(value, ALONG_X, pairs)


def column_halves(rows, axes):
    half = rows.shape[1] // 2
    for_core = jnp.stack([rows[:, :half], rows[:, half:]])
    reach = lax.axis_size(axes[0])
    copies = jnp.broadcast_to(for_core, (reach, *for_core.shape)).reshape(-1, *for_core.shape[1:])
    return lax.all_to_all(copies, axes, split_axis=0, concat_axis=0, tiled=True)


def compute(tokens, queries, positions, grad, master, moment1, moment2, step):
    head_dim = master.shape[1] // 2
    local_count = tokens.shape[0]
    core = lax.axis_index(CORE)
    place = jnp.stack([core, 2 * lax.axis_index(X_HI) + lax.axis_index("x_lo")]).astype(jnp.int32)
    new_master, new_first, new_second = adam_update(grad, master, moment1, moment2, step)
    weight = new_master.astype(jnp.bfloat16)
    over_z = column_halves(weight, (ALONG_Z, CORE)).reshape(-1, head_dim)
    mine = split_columns(tokens)
    theirs = lax.ppermute(mine, CORE, [(0, 1), (1, 0)])
    places_both = lax.all_gather(positions, CORE, axis=0, tiled=True)
    places_other = jnp.where(core == 0, places_both[local_count:], places_both[:local_count])
    cosine, sine = rotation_tables(positions, head_dim)
    cosine_other, sine_other = rotation_tables(places_other, head_dim)
    is_keys = core == 0
    key_cosine = jnp.where(is_keys, jnp.concatenate([cosine, cosine_other]), 1.0)
    key_sine = jnp.where(is_keys, jnp.concatenate([sine, sine_other]), 0.0)
    first = jnp.broadcast_to(
        (jnp.arange(local_count, dtype=jnp.int32) - positions)[:, None],
        (local_count, head_dim),
    )
    over_y = from_everyone(over_z, ALONG_Y).reshape(-1, head_dim)
    half = over_y.shape[0] // 2
    low, high = over_y[:half], over_y[half:]
    tiles = (2 * local_count, head_dim)
    left_low = along_x(low, 1)
    right_high = along_x(high, 3)
    left_high = along_x(high, 1)
    right_low = along_x(low, 3)
    so_far = product(own_kernel, place, tiles, jnp.float32, 1, mine, theirs, low, high)
    across_low = along_x(left_low, 1)
    across_high = along_x(right_high, 3)
    so_far = product(
        beside_kernel, place, tiles, jnp.float32, 2,
        so_far, mine, theirs, left_low, left_high, right_low, right_high,
    )
    half_kv = product(
        across_kernel, place, tiles, jnp.bfloat16, 1,
        so_far, mine, theirs, across_low, across_high, key_cosine, key_sine,
    )
    row_kv = lax.all_gather(half_kv, X_HI, axis=0, tiled=True)
    one_back = shifted(row_kv, CHIPS, 2)
    two_back = shifted(row_kv, CHIPS, 4)
    row_both = lax.all_gather(row_kv, CORE, axis=0)
    back_both = lax.all_gather(jnp.concatenate([two_back, one_back], axis=0), CORE, axis=0)
    offset = lax.axis_index(("x_hi", "core")) * local_count
    attention = attend(
        offset.astype(jnp.int32)[None], back_both, row_both, queries, first, cosine, sine
    )
    return (attention, new_master, new_first, new_second)


def solution(mesh):
    finer = Mesh(mesh.devices.reshape(2, 16, 8, 2, 2), EVERY)
    rows = P(EVERY, None)
    placed = (rows, rows, P(EVERY), rows, rows, rows, rows, P())
    return jax.shard_map(
        compute,
        mesh=finer,
        in_specs=placed,
        out_specs=(rows, rows, rows, rows),
        check_vma=False,
    )
```

time: 130 us -> 122 us (0.938)
  blocking collectives: 68.1 us -> 46 us
  waiting for transfers between devices: 18 us -> 24.1 us
  Pallas kernels: 8.1 us -> 12.2 us
  starting transfers between devices: 28.5 us -> 31.8 us
  other arithmetic: 1.07 us -> 3.16 us
    all_gather x5 -> x4, blocking collectives: 68.1 us -> 12.6 us  [the longest x1 6.57 us: compute(): row_kv = lax.all_gather(half_kv, X_HI, axis=0, tiled=True)]
    all_to_all x0 -> x1, blocking collectives: none -> 33.4 us  [column_halves(): return lax.all_to_all(copies, axes, split_axis=0, concat_axis=0, tiled=True)]
    ppermute x0 -> x7, starting transfers between devices: none -> 20.3 us  [the longest x6 18.4 us: along_x(): return lax.ppermute(value, ALONG_X, pairs)]
    all_to_all x2 -> x1, starting transfers between devices: 21.8 us -> 7.1 us  [from_everyone(): return lax.all_to_all(copies, axis, split_axis=0, concat_axis=0, tiled=True)]
    all_to_all x2 -> x1, waiting for transfers between devices: 10 us -> 14.7 us  [from_everyone(): return lax.all_to_all(copies, axis, split_axis=0, concat_axis=0, tiled=True)]
    pallas_call x3 -> x4, Pallas kernels: 3.24 us -> 7.35 us  [the longest x3 6.5 us: product(): pl.pallas_call(kernel, out_shape=jax.ShapeDtypeStruct(tiles, dtype), in_s...]
    ppermute x2, starting transfers between devices: 6.73 us -> 4.38 us  [shifted(): lax.ppermute(value, axis, [(source, source + steps) for source in range(c...]
    ppermute x0 -> x7, waiting for transfers between devices: none -> 1.94 us  [the longest x6 1.93 us: along_x(): return lax.ppermute(value, ALONG_X, pairs)]
  transfers between devices with their start and end apart: 4 -> 10, of which waited for: 3 -> 4; matrix products, arithmetic and copies ran while one was open for 1% -> 3% of each run, Pallas kernels for 0% -> 4%
where the time goes in v1:
time: 122 us; the launch traced here: 121 us
  blocking collectives  46 us (38%)
  starting transfers between devices  31.8 us (26%)
  waiting for transfers between devices  24.1 us (20%)
  Pallas kernels  12.2 us (10%)
  other arithmetic  3.16 us (3%)
  local copies, waits for them, and re-layouts  2.6 us (2%)
  between operations  1.61 us (1%)
    all_to_all x1, blocking collectives, column_halves(): return lax.all_to_all(copies, axes, split_axis=0, concat_axis=0, tiled=True)  33.4 us
    ppermute x6, starting transfers between devices, along_x(): return lax.ppermute(value, ALONG_X, pairs)  18.4 us
    all_to_all x1, waiting for transfers between devices, from_everyone(): return lax.all_to_all(copies, axis, split_axis=0, concat_axis=0, tiled=True)  14.7 us
    ppermute x2, waiting for transfers between devices, shifted(): lax.ppermute(value, axis, [(source, source + steps) for source in range(c...  7.37 us
    all_to_all x1, starting transfers between devices, from_everyone(): return lax.all_to_all(copies, axis, split_axis=0, concat_axis=0, tiled=True)  7.1 us
    all_gather x1, blocking collectives, compute(): row_kv = lax.all_gather(half_kv, X_HI, axis=0, tiled=True)  6.57 us
    pallas_call x3, Pallas kernels, product(): pl.pallas_call(kernel, out_shape=jax.ShapeDtypeStruct(tiles, dtype), in_s...  6.5 us
    pallas_call x1, Pallas kernels, attend(): pl.pallas_call(attend_kernel, out_shape=jax.ShapeDtypeStruct((count, widt...  4.86 us
  transfers between devices with their start and end apart: 10, of which 4 were waited for; matrix products, arithmetic and copies ran while one was open for 3% of the time, Pallas kernels for 4%

profile of v1, /device:TPU:6, one launch (start us, length us, event | category | flops | bytes accessed | tf_op | source)
XLA Modules:
  0.0 121.4 jit_solution(4187131456148262266)
XLA Ops:
  0.6 0.0 copy-start
  0.6 1.6 %copy-done = bf16[128,8192]{1,0:T(8,128)(2,1)S(1)} copy-done((bf16[128,8192]{1,0:T(8,128)(2,1)S(1)}, bf16[128,8192]{1,0:T(8,128)(2,1)}, u32[]{:S(2)}) %copy-start) | copy-done | bytes 2097176
  2.2 0.0 copy-start.7
  2.2 0.8 shard_map.111.mine_ref
  3.1 1.9 %collective-permute-start = (bf16[4,128,2048]{2,1,0:T(8,128)(2,1)S(1)}, bf16[4,128,2048]{2,1,0:T(8,128)(2,1)}, u32[]{:S(2)}, u32[]{:S(2)}) collective-permute-start(bf16[4,128,2048]{2,1,0:T(8,128)(2,1)S(1)} %shard_map.111.mine_ref), channel_id=1, source_target_pairs={{0,1},{1,0},{2,3},{3,2},{4,5},{5,4},{6,7},{7,6},{8,9},{9,8},{10,11... | collective-permute-start | bytes 6291464 | tf_op jit(solution)/shard_map/ppermute | solution.py:267
  5.8 0.0 copy-done.3
  5.8 0.0 copy-done.4
  5.8 0.0 copy-done.5
  5.8 0.0 copy-done.6
  5.8 0.6 fusion.5
  6.5 33.4 %all_to_all.10 = bf16[32,8,128]{2,1,0:T(8,128)(2,1)S(1)} all-to-all(bf16[32,8,128]{2,1,0:T(8,128)(2,1)S(1)} %bitcast.27), channel_id=1, replica_groups=mesh['x_lo'=2,'z'=16,'y'=8,'x_hi'=2,'core'=2] {'z','core'}, dimensions={0} | all-to-all | bytes 131072 | tf_op jit(solution)/shard_map/all_to_all | solution.py:255
  39.9 0.9 broadcast_in_dim.28
  40.7 7.1 %all-to-all-start.1 = ((bf16[8,256,128]{2,1,0:T(8,128)(2,1)}), bf16[8,256,128]{2,1,0:T(8,128)(2,1)S(1)}, u32[]{:S(2)}, u32[]{:S(2)}) async-start(bf16[8,256,128]{2,1,0:T(8,128)(2,1)} %broadcast_in_dim.28), calls=%async_computation.1 | async-start | bytes 1048576 | tf_op jit(solution)/shard_map/all_to_all | solution.py:31
  47.8 0.0 copy-done.7
  47.9 1.8 %all-gather.2 = s32[2,1,128]{2,1,0:T(1,128)S(1)} all-gather(s32[1,1,128]{2,1,0:T(1,128)S(1)} %bitcast.28), channel_id=1, replica_groups=mesh['x_lo'=2,'z'=16,'y'=8,'x_hi'=2,'core'=2] {'core'}, dimensions={0}, use_global_device_ids=true | all-gather | bytes 1536 | tf_op jit(solution)/shard_map/all_gather | solution.py:268
  49.7 14.7 %all-to-all-done.1 = bf16[8,256,128]{2,1,0:T(8,128)(2,1)S(1)} async-done(((bf16[8,256,128]{2,1,0:T(8,128)(2,1)}), bf16[8,256,128]{2,1,0:T(8,128)(2,1)S(1)}, u32[]{:S(2)}, u32[]{:S(2)}) %all-to-all-start.1) | async-done | bytes 524320 | tf_op jit(solution)/shard_map/all_to_all | solution.py:31
  64.5 2.4 %collective-permute-start.1 = (bf16[1024,128]{1,0:T(8,128)(2,1)S(1)}, bf16[1024,128]{1,0:T(8,128)(2,1)S(1)}, u32[]{:S(2)}, u32[]{:S(2)}) collective-permute-start(bf16[1024,128]{1,0:T(8,128)(2,1)S(1)} %bitcast.18), channel_id=1, source_target_pairs={{0,512},{2,514},{512,2},{514,0},{1,513},{3,515},{513,3},{515,1},{4... | collective-permute-start | bytes 786440 | tf_op jit(solution)/shard_map/ppermute | solution.py:247
  66.8 3.5 %collective-permute-start.4 = (bf16[1024,128]{1,0:T(8,128)(2,1)S(1)}, bf16[1024,128]{1,0:T(8,128)(2,1)S(1)}, u32[]{:S(2)}, u32[]{:S(2)}) collective-permute-start(bf16[1024,128]{1,0:T(8,128)(2,1)S(1)} %bitcast.21), channel_id=1, source_target_pairs={{0,514},{2,512},{512,0},{514,2},{1,515},{3,513},{513,1},{515,3},{4... | collective-permute-start | bytes 786440 | tf_op jit(solution)/shard_map/ppermute | solution.py:247
  70.3 3.6 %collective-permute-start.2 = (bf16[1024,128]{1,0:T(8,128)(2,1)S(1)}, bf16[1024,128]{1,0:T(8,128)(2,1)S(1)}, u32[]{:S(2)}, u32[]{:S(2)}) collective-permute-start(bf16[1024,128]{1,0:T(8,128)(2,1)S(1)} %bitcast.22), channel_id=1, source_target_pairs={{0,512},{2,514},{512,2},{514,0},{1,513},{3,515},{513,3},{515,1},{4... | collective-permute-start | bytes 786440 | tf_op jit(solution)/shard_map/ppermute | solution.py:247
  73.9 2.2 %collective-permute-start.3 = (bf16[1024,128]{1,0:T(8,128)(2,1)S(1)}, bf16[1024,128]{1,0:T(8,128)(2,1)}, u32[]{:S(2)}, u32[]{:S(2)}) collective-permute-start(bf16[1024,128]{1,0:T(8,128)(2,1)S(1)} %bitcast.19), channel_id=1, source_target_pairs={{0,514},{2,512},{512,0},{514,2},{1,515},{3,513},{513,1},{515,3},{4... | collective-permute-start | bytes 786440 | tf_op jit(solution)/shard_map/ppermute | solution.py:247
  76.2 1.2 fusion
  77.4 0.0 collective-permute-done.1.pieces_and_out_0_
  77.4 4.8 %collective-permute-start.5 = (bf16[1024,128]{1,0:T(8,128)(2,1)S(1)}, bf16[1024,128]{1,0:T(8,128)(2,1)S(1)}, u32[]{:S(2)}, u32[]{:S(2)}) collective-permute-start(bf16[1024,128]{1,0:T(8,128)(2,1)S(1)} %collective-permute-done.1.pieces_and_out_0_), channel_id=1, source_target_pairs={{0,512},{2,514},{512,2},{514,0},{1,513},{3,515},{513,3},{515,1},{4... | collective-permute-start | bytes 786440 | tf_op jit(solution)/shard_map/ppermute | solution.py:247
  82.2 0.0 collective-permute-done.4.pieces_and_out_3_
  82.2 1.9 %collective-permute-start.6 = (bf16[1024,128]{1,0:T(8,128)(2,1)S(1)}, bf16[1024,128]{1,0:T(8,128)(2,1)S(1)}, u32[]{:S(2)}, u32[]{:S(2)}) collective-permute-start(bf16[1024,128]{1,0:T(8,128)(2,1)S(1)} %collective-permute-done.4.pieces_and_out_3_), channel_id=1, source_target_pairs={{0,514},{2,512},{512,0},{514,2},{1,515},{3,513},{513,1},{515,3},{4... | collective-permute-start | bytes 786440 | tf_op jit(solution)/shard_map/ppermute | solution.py:247
  84.1 0.1 pad_add_fusion.place_ref
  84.2 1.1 maximum_select_fusion
  85.3 0.0 collective-permute-done.theirs_ref
  85.3 2.0 %shard_map.112.so_far_ref = f32[256,128]{1,0:T(8,128)S(1)} custom-call(s32[2]{0:T(128)S(1)} %pad_add_fusion.place_ref, bf16[4,128,2048]{2,1,0:T(8,128)(2,1)S(1)} %shard_map.111.mine_ref, bf16[4,128,2048]{2,1,0:T(8,128)(2,1)} %collective-permute-done.theirs_ref, bf16[1024,128]{1,0:T(8,128)(2,1)S(1)} %bitcast.20, bf16[1024,128]{1,0:T(8,128)(2,1)S(1)} %bitcast.23), custom_call_target="tpu_custom_call" | custom-call | flops 134217728 | bytes 1572864 | tf_op jit(solution)/shard_map/pallas_call | solution.py:139
  87.4 0.0 collective-permute-done.2.pieces_and_out_1_
  87.4 0.0 collective-permute-done.3.pieces_and_out_2_
  87.4 2.3 %shard_map.113.so_far_ref = f32[256,128]{1,0:T(8,128)S(1)} custom-call(s32[2]{0:T(128)S(1)} %pad_add_fusion.place_ref, f32[256,128]{1,0:T(8,128)S(1)} %shard_map.112.so_far_ref, bf16[4,128,2048]{2,1,0:T(8,128)(2,1)S(1)} %shard_map.111.mine_ref, bf16[4,128,2048]{2,1,0:T(8,128)(2,1)} %collective-permute-done.theirs_ref, ...), custom_call_target="tpu_custom_call" | custom-call | flops 268435456 | bytes 3145728 | tf_op jit(solution)/shard_map/pallas_call | solution.py:139
  89.7 0.0 collective-permute-done.5.low_ref
  89.7 1.9 %collective-permute-done.6.high_ref = bf16[1024,128]{1,0:T(8,128)(2,1)S(1)} collective-permute-done((bf16[1024,128]{1,0:T(8,128)(2,1)S(1)}, bf16[1024,128]{1,0:T(8,128)(2,1)S(1)}, u32[]{:S(2)}, u32[]{:S(2)}) %collective-permute-start.6) | collective-permute-done | bytes 262176 | tf_op jit(solution)/shard_map/ppermute | solution.py:247
  91.7 2.1 %shard_map.114 = bf16[256,128]{1,0:T(8,128)(2,1)S(1)} custom-call(s32[2]{0:T(128)S(1)} %pad_add_fusion.place_ref, f32[256,128]{1,0:T(8,128)S(1)} %shard_map.113.so_far_ref, bf16[4,128,2048]{2,1,0:T(8,128)(2,1)S(1)} %shard_map.111.mine_ref, bf16[4,128,2048]{2,1,0:T(8,128)(2,1)} %collective-permute-done.theirs_ref, ...), custom_call_target="tpu_custom_call" | custom-call | flops 134217728 | bytes 1572864 | tf_op jit(solution)/shard_map/pallas_call | solution.py:139
  93.8 0.0 copy-start.1
  93.8 6.6 %all_gather.19 = bf16[512,128]{1,0:T(8,128)(2,1)S(1)} all-gather(bf16[256,128]{1,0:T(8,128)(2,1)S(1)} %shard_map.114), channel_id=1, replica_groups=mesh['x_lo'=2,'z'=16,'y'=8,'x_hi'=2,'core'=2] {'x_hi'}, dimensions={0}, use_global_device_ids=true | all-gather | bytes 196608 | tf_op jit(solution)/shard_map/all_gather | solution.py:298
  100.4 1.9 %collective-permute-start.7 = (bf16[512,128]{1,0:T(8,128)(2,1)S(1)}, bf16[512,128]{1,0:T(8,128)(2,1)S(1)}, u32[]{:S(2)}, u32[]{:S(2)}) collective-permute-start(bf16[512,128]{1,0:T(8,128)(2,1)S(1)} %all_gather.19), channel_id=1, source_target_pairs={{0,8},{2,10},{4,12},{6,14},{8,16},{10,18},{12,20},{14,22},{16,24},... | collective-permute-start | bytes 393224 | tf_op jit(solution)/shard_map/ppermute | solution.py:238
  102.3 2.5 %collective-permute-start.8 = (bf16[512,128]{1,0:T(8,128)(2,1)S(1)}, bf16[512,128]{1,0:T(8,128)(2,1)S(1)}, u32[]{:S(2)}, u32[]{:S(2)}) collective-permute-start(bf16[512,128]{1,0:T(8,128)(2,1)S(1)} %all_gather.19), channel_id=1, source_target_pairs={{0,4},{2,6},{4,8},{6,10},{8,12},{10,14},{12,16},{14,18},{16,20},{1... | collective-permute-start | bytes 393224 | tf_op jit(solution)/shard_map/ppermute | solution.py:238
  104.8 0.0 copy-done.2
  104.8 0.1 pad_maximum_fusion.1
  104.9 2.0 %all-gather.1 = bf16[1024,128]{1,0:T(8,128)(2,1)S(1)} all-gather(bf16[512,128]{1,0:T(8,128)(2,1)S(1)} %all_gather.19), channel_id=3, replica_groups=mesh['x_lo'=2,'z'=16,'y'=8,'x_hi'=2,'core'=2] {'core'}, dimensions={0}, use_global_device_ids=true | all-gather | bytes 393216 | tf_op jit(solution)/shard_map/all_gather | solution.py:301
  106.9 6.5 %collective-permute-done.7 = bf16[512,128]{1,0:T(8,128)(2,1)S(1)} collective-permute-done((bf16[512,128]{1,0:T(8,128)(2,1)S(1)}, bf16[512,128]{1,0:T(8,128)(2,1)S(1)}, u32[]{:S(2)}, u32[]{:S(2)}) %collective-permute-start.7) | collective-permute-done | bytes 131104 | tf_op jit(solution)/shard_map/ppermute | solution.py:238
  113.4 0.8 collective-permute-done.8
  114.3 2.2 %all-gather = bf16[2048,128]{1,0:T(8,128)(2,1)S(1)} all-gather(bf16[1024,128]{1,0:T(8,128)(2,1)S(1)} %pad_maximum_fusion), channel_id=2, replica_groups=mesh['x_lo'=2,'z'=16,'y'=8,'x_hi'=2,'core'=2] {'core'}, dimensions={0}, use_global_device_ids=true | all-gather | bytes 786432 | tf_op jit(solution)/shard_map/all_gather | solution.py:302
  116.5 0.1 broadcast_in_dim.31.first_ref
  116.5 0.0 copy-done.1
  116.6 4.9 %shard_map.115 = bf16[128,1024]{1,0:T(8,128)(2,1)} custom-call(s32[1]{0:T(128)} %bitcast.offset_ref, bf16[2,1024,128]{2,1,0:T(8,128)(2,1)S(1)} %bitcast.24, bf16[2,512,128]{2,1,0:T(8,128)(2,1)S(1)} %bitcast.25, bf16[128,1024]{1,0:T(8,128)(2,1)S(1)} %copy-done.1, s32[128,128]{1,0:T(8,128)S(1)} %broadcast_in_dim.31.first_ref, ...), custom_call_target="tpu_custom_call" | custom-call | flops 603979776 | bytes 1310720 | tf_op jit(solution)/shard_map/pallas_call | solution.py:207
  (13 shorter events, 0.1 us)
Async XLA Ops:
  0.6 1.6 %copy-start = (bf16[128,8192]{1,0:T(8,128)(2,1)S(1)}, bf16[128,8192]{1,0:T(8,128)(2,1)}, u32[]{:S(2)}) copy-start(bf16[128,8192]{1,0:T(8,128)(2,1)} %tokens_ref.1) | copy-start | bytes 6291460
  2.2 3.5 %copy-start.3 = (f32[8,256]{1,0:T(8,128)S(1)}, f32[8,256]{1,0:T(8,128)}, u32[]{:S(2)}) copy-start(f32[8,256]{1,0:T(8,128)} %param.12) | copy-start | bytes 24580
  2.2 3.5 %copy-start.4 = (f32[8,256]{1,0:T(8,128)S(1)}, f32[8,256]{1,0:T(8,128)}, u32[]{:S(2)}) copy-start(f32[8,256]{1,0:T(8,128)} %param.11) | copy-start | bytes 24580
  2.2 3.6 %copy-start.5 = (f32[8,256]{1,0:T(8,128)S(1)}, f32[8,256]{1,0:T(8,128)}, u32[]{:S(2)}) copy-start(f32[8,256]{1,0:T(8,128)} %param.13) | copy-start | bytes 24580
  2.2 3.6 %copy-start.6 = (f32[8,256]{1,0:T(8,128)S(1)}, f32[8,256]{1,0:T(8,128)}, u32[]{:S(2)}) copy-start(f32[8,256]{1,0:T(8,128)} %param.14) | copy-start | bytes 24580
  2.2 45.6 %copy-start.7 = (s32[128]{0:T(128)S(1)}, s32[128]{0:T(128)}, u32[]{:S(2)}) copy-start(s32[128]{0:T(128)} %param.10) | copy-start | bytes 1540
  3.1 82.2 %collective-permute-start = (bf16[4,128,2048]{2,1,0:T(8,128)(2,1)S(1)}, bf16[4,128,2048]{2,1,0:T(8,128)(2,1)}, u32[]{:S(2)}, u32[]{:S(2)}) collective-permute-start(bf16[4,128,2048]{2,1,0:T(8,128)(2,1)S(1)} %shard_map.111.mine_ref), channel_id=1, source_target_pairs={{0,1},{1,0},{2,3},{3,2},{4,5},{5,4},{6,7},{7,6},{8,9},{9,8},{10,11... | collective-permute-start | bytes 6291464 | tf_op jit(solution)/shard_map/ppermute | solution.py:267
  40.7 23.7 %all-to-all-start.1 = ((bf16[8,256,128]{2,1,0:T(8,128)(2,1)}), bf16[8,256,128]{2,1,0:T(8,128)(2,1)S(1)}, u32[]{:S(2)}, u32[]{:S(2)}) async-start(bf16[8,256,128]{2,1,0:T(8,128)(2,1)} %broadcast_in_dim.28), calls=%async_computation.1 | async-start | bytes 1048576 | tf_op jit(solution)/shard_map/all_to_all | solution.py:31
  64.5 12.9 %collective-permute-start.1 = (bf16[1024,128]{1,0:T(8,128)(2,1)S(1)}, bf16[1024,128]{1,0:T(8,128)(2,1)S(1)}, u32[]{:S(2)}, u32[]{:S(2)}) collective-permute-start(bf16[1024,128]{1,0:T(8,128)(2,1)S(1)} %bitcast.18), channel_id=1, source_target_pairs={{0,512},{2,514},{512,2},{514,0},{1,513},{3,515},{513,3},{515,1},{4... | collective-permute-start | bytes 786440 | tf_op jit(solution)/shard_map/ppermute | solution.py:247
  66.8 15.3 %collective-permute-start.4 = (bf16[1024,128]{1,0:T(8,128)(2,1)S(1)}, bf16[1024,128]{1,0:T(8,128)(2,1)S(1)}, u32[]{:S(2)}, u32[]{:S(2)}) collective-permute-start(bf16[1024,128]{1,0:T(8,128)(2,1)S(1)} %bitcast.21), channel_id=1, source_target_pairs={{0,514},{2,512},{512,0},{514,2},{1,515},{3,513},{513,1},{515,3},{4... | collective-permute-start | bytes 786440 | tf_op jit(solution)/shard_map/ppermute | solution.py:247
  70.3 17.1 %collective-permute-start.2 = (bf16[1024,128]{1,0:T(8,128)(2,1)S(1)}, bf16[1024,128]{1,0:T(8,128)(2,1)S(1)}, u32[]{:S(2)}, u32[]{:S(2)}) collective-permute-start(bf16[1024,128]{1,0:T(8,128)(2,1)S(1)} %bitcast.22), channel_id=1, source_target_pairs={{0,512},{2,514},{512,2},{514,0},{1,513},{3,515},{513,3},{515,1},{4... | collective-permute-start | bytes 786440 | tf_op jit(solution)/shard_map/ppermute | solution.py:247
  73.9 13.5 %collective-permute-start.3 = (bf16[1024,128]{1,0:T(8,128)(2,1)S(1)}, bf16[1024,128]{1,0:T(8,128)(2,1)}, u32[]{:S(2)}, u32[]{:S(2)}) collective-permute-start(bf16[1024,128]{1,0:T(8,128)(2,1)S(1)} %bitcast.19), channel_id=1, source_target_pairs={{0,514},{2,512},{512,0},{514,2},{1,515},{3,513},{513,1},{515,3},{4... | collective-permute-start | bytes 786440 | tf_op jit(solution)/shard_map/ppermute | solution.py:247
  77.4 12.4 %collective-permute-start.5 = (bf16[1024,128]{1,0:T(8,128)(2,1)S(1)}, bf16[1024,128]{1,0:T(8,128)(2,1)S(1)}, u32[]{:S(2)}, u32[]{:S(2)}) collective-permute-start(bf16[1024,128]{1,0:T(8,128)(2,1)S(1)} %collective-permute-done.1.pieces_and_out_0_), channel_id=1, source_target_pairs={{0,512},{2,514},{512,2},{514,0},{1,513},{3,515},{513,3},{515,1},{4... | collective-permute-start | bytes 786440 | tf_op jit(solution)/shard_map/ppermute | solution.py:247
  82.2 9.5 %collective-permute-start.6 = (bf16[1024,128]{1,0:T(8,128)(2,1)S(1)}, bf16[1024,128]{1,0:T(8,128)(2,1)S(1)}, u32[]{:S(2)}, u32[]{:S(2)}) collective-permute-start(bf16[1024,128]{1,0:T(8,128)(2,1)S(1)} %collective-permute-done.4.pieces_and_out_3_), channel_id=1, source_target_pairs={{0,514},{2,512},{512,0},{514,2},{1,515},{3,513},{513,1},{515,3},{4... | collective-permute-start | bytes 786440 | tf_op jit(solution)/shard_map/ppermute | solution.py:247
  91.7 13.1 %copy-start.2 = (f32[128,64]{1,0:T(8,128)S(1)}, f32[128,64]{1,0:T(8,128)}, u32[]{:S(2)}) copy-start(f32[128,64]{1,0:T(8,128)} %get-tuple-element.14) | copy-start | bytes 98308
  93.8 22.7 %copy-start.1 = (bf16[128,1024]{1,0:T(8,128)(2,1)S(1)}, bf16[128,1024]{1,0:T(8,128)(2,1)}, u32[]{:S(2)}) copy-start(bf16[128,1024]{1,0:T(8,128)(2,1)} %queries_ref.1) | copy-start | bytes 786436
  100.4 13.0 %collective-permute-start.7 = (bf16[512,128]{1,0:T(8,128)(2,1)S(1)}, bf16[512,128]{1,0:T(8,128)(2,1)S(1)}, u32[]{:S(2)}, u32[]{:S(2)}) collective-permute-start(bf16[512,128]{1,0:T(8,128)(2,1)S(1)} %all_gather.19), channel_id=1, source_target_pairs={{0,8},{2,10},{4,12},{6,14},{8,16},{10,18},{12,20},{14,22},{16,24},... | collective-permute-start | bytes 393224 | tf_op jit(solution)/shard_map/ppermute | solution.py:238
  102.3 12.0 %collective-permute-start.8 = (bf16[512,128]{1,0:T(8,128)(2,1)S(1)}, bf16[512,128]{1,0:T(8,128)(2,1)S(1)}, u32[]{:S(2)}, u32[]{:S(2)}) collective-permute-start(bf16[512,128]{1,0:T(8,128)(2,1)S(1)} %all_gather.19), channel_id=1, source_target_pairs={{0,4},{2,6},{4,8},{6,10},{8,12},{10,14},{12,16},{14,18},{16,20},{1... | collective-permute-start | bytes 393224 | tf_op jit(solution)/shard_map/ppermute | solution.py:238

commit v2 on v1

--- a/solution.py
+++ b/solution.py
@@ -87,46 +87,47 @@
     )(tokens)
 
 
-def plane_product(mine_ref, theirs_ref, plane, halves, columns):
-    depth = 16
-    for half, half_ref in enumerate(halves):
-        for y in range(4):
+def plane_product(mine_ref, theirs_ref, plane, pieces, columns, held, arrival):
+    fetch = pltpu.make_async_copy(theirs_ref.at[plane], held, arrival)
+    fetch.start()
+    depth, along_y = 16, 8 // len(pieces)
+    for order, piece_ref in enumerate(pieces):
+        for y in range(along_y):
             for z in range(16):
-                place = (z * 8 + 4 * half + y) * depth
-                columns[place : place + depth] = half_ref[
+                place = (z * 8 + along_y * order + y) * depth
+                columns[place : place + depth] = piece_ref[
                     (y * 16 + z) * depth : (y * 16 + z + 1) * depth
                 ]
-    rows = jnp.concatenate([mine_ref[plane], theirs_ref[plane]], axis=0)
-    return jnp.dot(rows, columns[...], preferred_element_type=jnp.float32)
-
-
-def own_kernel(place_ref, mine_ref, theirs_ref, low_ref, high_ref, out_ref, columns):
+    own = jnp.dot(mine_ref[plane], columns[...], preferred_element_type=jnp.float32)
+    fetch.wait()
+    other = jnp.dot(held[...], columns[...], preferred_element_type=jnp.float32)
+    return jnp.concatenate([own, other], axis=0)
+
+
+def own_kernel(place_ref, theirs_ref, mine_ref, piece_ref, out_ref, columns, held, arrival):
     out_ref[...] = plane_product(
-        mine_ref, theirs_ref, place_ref[1], (low_ref, high_ref), columns
+        mine_ref, theirs_ref, place_ref[1], (piece_ref,), columns, held, arrival
     )
 
 
 def beside_kernel(
-    place_ref, so_far_ref, mine_ref, theirs_ref, *pieces_and_out
+    place_ref, theirs_ref, mine_ref, so_far_ref, left_ref, right_ref, out_ref, *scratches
 ):
-    left_low, left_high, right_low, right_high, out_ref, columns, more = pieces_and_out
     left = (place_ref[1] + 3) & 3
     right = (place_ref[1] + 1) & 3
-    out_ref[...] = (
-        so_far_ref[...]
-        + plane_product(mine_ref, theirs_ref, left, (left_low, left_high), columns)
-        + plane_product(mine_ref, theirs_ref, right, (right_low, right_high), more)
-    )
+    from_left = plane_product(mine_ref, theirs_ref, left, (left_ref,), *scratches[0::2])
+    from_right = plane_product(mine_ref, theirs_ref, right, (right_ref,), *scratches[1::2])
+    out_ref[...] = so_far_ref[...] + from_left + from_right
 
 
 def across_kernel(
-    place_ref, so_far_ref, mine_ref, theirs_ref, low_ref, high_ref, cosine_ref, sine_ref,
-    out_ref, columns,
+    place_ref, theirs_ref, mine_ref, so_far_ref, low_ref, high_ref, cosine_ref, sine_ref,
+    out_ref, columns, held, arrival,
 ):
     across = (place_ref[1] + 2) & 3
     core = place_ref[0]
     total = so_far_ref[...] + plane_product(
-        mine_ref, theirs_ref, across, (low_ref, high_ref), columns
+        mine_ref, theirs_ref, across, (low_ref, high_ref), columns, held, arrival
     )
     count = mine_ref.shape[1]
     done = turned(total, cosine_ref[...], sine_ref[...]).astype(jnp.bfloat16)
@@ -134,21 +135,30 @@
     out_ref[pl.ds(pl.multiple_of((1 - core) * count, count), count)] = done[count:]
 
 
-def product(kernel, place, tiles, dtype, scratches, *operands):
+def product(kernel, place, theirs, mine, tiles, dtype, planes, *operands):
     rows, width = tiles
+    depth = mine.shape[2]
     return pl.pallas_call(
         kernel,
         out_shape=jax.ShapeDtypeStruct(tiles, dtype),
-        in_specs=[pl.BlockSpec(memory_space=pltpu.SMEM), *on_chip(len(operands))],
+        in_specs=[
+            pl.BlockSpec(memory_space=pltpu.SMEM),
+            pl.BlockSpec(memory_space=pl.ANY),
+            *on_chip(len(operands) + 1),
+        ],
         out_specs=on_chip(1)[0],
-        scratch_shapes=[pltpu.VMEM((2048, width), jnp.bfloat16)] * scratches,
+        scratch_shapes=[
+            *[pltpu.VMEM((depth, width), jnp.bfloat16)] * planes,
+            *[pltpu.VMEM(mine.shape[1:], jnp.bfloat16)] * planes,
+            *[pltpu.SemaphoreType.DMA] * planes,
+        ],
         compiler_params=room(8),
         cost_estimate=pl.CostEstimate(
-            flops=2 * rows * width * 2048 * scratches,
-            bytes_accessed=2 * 2048 * (rows + width) * scratches,
+            flops=2 * rows * width * depth * planes,
+            bytes_accessed=2 * depth * (rows + width) * planes,
             transcendentals=0,
         ),
-    )(place, *operands)
+    )(place, theirs, mine, *operands)
 
 
 def turned(values, cosine, sine):
@@ -156,16 +166,17 @@
 
 
 def attend_kernel(
-    offset_ref, back_ref, row_ref, queries_ref, first_ref, cosine_ref, sine_ref, out_ref, *windows
+    offset_ref, far_ref, near_ref, queries_ref, first_ref, cosine_ref, sine_ref, out_ref, *windows
 ):
     count, width = queries_ref.shape
     head_dim = cosine_ref.shape[1]
-    reach = back_ref.shape[1]
-    seen = reach + count
+    held = far_ref.shape[1]
+    seen = windows[0].shape[0] - count
+    reach = seen - count
     near = pl.ds(pl.multiple_of(offset_ref[0], 128), seen)
     for kind, window in enumerate(windows):
-        window[:reach] = back_ref[kind]
-        window[reach:] = row_ref[kind]
+        window[:held] = far_ref[kind]
+        window[held:] = near_ref[kind]
     keys, values = (window[near] for window in windows)
     row = lax.broadcasted_iota(jnp.int32, (count, head_dim), 0)
     column = lax.broadcasted_iota(jnp.int32, (count, head_dim), 1)
@@ -202,21 +213,21 @@
         ).astype(jnp.bfloat16)
 
 
-def attend(offset, back, row, queries, first, cosine, sine):
+def attend(offset, far, close, queries, first, cosine, sine):
     count, width = queries.shape
     return pl.pallas_call(
         attend_kernel,
         out_shape=jax.ShapeDtypeStruct((count, width), jnp.bfloat16),
         in_specs=[pl.BlockSpec(memory_space=pltpu.SMEM), *on_chip(6)],
         out_specs=on_chip(1)[0],
-        scratch_shapes=[pltpu.VMEM((back.shape[1] + row.shape[1], row.shape[2]), jnp.bfloat16)] * 2,
+        scratch_shapes=[pltpu.VMEM((far.shape[1] + close.shape[1], close.shape[2]), jnp.bfloat16)] * 2,
         compiler_params=room(20),
         cost_estimate=pl.CostEstimate(
             flops=4 * count * width * 1152,
-            bytes_accessed=4 * count * width + 2 * back.size + 2 * row.size,
+            bytes_accessed=4 * count * width + 2 * far.size + 2 * close.size,
             transcendentals=count * width * 9,
         ),
-    )(offset, back, row, queries, first, cosine, sine)
+    )(offset, far, close, queries, first, cosine, sine)
 
 
 def rotation_tables(places, head_dim):
@@ -278,31 +289,28 @@
     )
     over_y = from_everyone(over_z, ALONG_Y).reshape(-1, head_dim)
     half = over_y.shape[0] // 2
-    low, high = over_y[:half], over_y[half:]
     tiles = (2 * local_count, head_dim)
-    left_low = along_x(low, 1)
-    right_high = along_x(high, 3)
-    left_high = along_x(high, 1)
-    right_low = along_x(low, 3)
-    so_far = product(own_kernel, place, tiles, jnp.float32, 1, mine, theirs, low, high)
-    across_low = along_x(left_low, 1)
-    across_high = along_x(right_high, 3)
-    so_far = product(
-        beside_kernel, place, tiles, jnp.float32, 2,
-        so_far, mine, theirs, left_low, left_high, right_low, right_high,
-    )
+    left = along_x(over_y, 1)
+    right = along_x(over_y, 3)
+    so_far = product(own_kernel, place, theirs, mine, tiles, jnp.float32, 1, over_y)
+    across_low = along_x(left[:half], 1)
+    across_high = along_x(right[half:], 3)
+    so_far = product(beside_kernel, place, theirs, mine, tiles, jnp.float32, 2, so_far, left, right)
     half_kv = product(
-        across_kernel, place, tiles, jnp.bfloat16, 1,
-        so_far, mine, theirs, across_low, across_high, key_cosine, key_sine,
-    )
-    row_kv = lax.all_gather(half_kv, X_HI, axis=0, tiled=True)
-    one_back = shifted(row_kv, CHIPS, 2)
-    two_back = shifted(row_kv, CHIPS, 4)
-    row_both = lax.all_gather(row_kv, CORE, axis=0)
-    back_both = lax.all_gather(jnp.concatenate([two_back, one_back], axis=0), CORE, axis=0)
-    offset = lax.axis_index(("x_hi", "core")) * local_count
+        across_kernel, place, theirs, mine, tiles, jnp.bfloat16, 1,
+        so_far, across_low, across_high, key_cosine, key_sine,
+    )
+    one_back = shifted(half_kv, CHIPS, 1)
+    two_back = shifted(half_kv, CHIPS, 2)
+    near_half = jnp.concatenate([two_back, one_back], axis=0)
+    far_half = shifted(near_half, CHIPS, 2)
+    near_both = lax.all_gather(
+        jnp.concatenate([near_half, half_kv], axis=0), CORE, axis=0
+    )
+    far_both = lax.all_gather(far_half, CORE, axis=0)
+    offset = core * local_count
     attention = attend(
-        offset.astype(jnp.int32)[None], back_both, row_both, queries, first, cosine, sine
+        offset.astype(jnp.int32)[None], far_both, near_both, queries, first, cosine, sine
     )
     return (attention, new_master, new_first, new_second)
 

time: 122 us -> 127 us (1.041)
  the two profiles are of different devices: /device:TPU:6 before, /device:TPU:3 now
where the time goes in v2:
time: 127 us; the launch traced here: 126 us
  blocking collectives  51.5 us (41%)
  starting transfers between devices  28.1 us (22%)
  waiting for transfers between devices  27.5 us (22%)
  Pallas kernels  13.4 us (11%)
  local copies, waits for them, and re-layouts  2.59 us (2%)
  between operations  1.63 us (1%)
  other arithmetic  1.53 us (1%)
    all_to_all x1, blocking collectives, column_halves(): return lax.all_to_all(copies, axes, split_axis=0, concat_axis=0, tiled=True)  31.8 us
    all_to_all x1, waiting for transfers between devices, from_everyone(): return lax.all_to_all(copies, axis, split_axis=0, concat_axis=0, tiled=True)  12.6 us
    ppermute x4, starting transfers between devices, along_x(): return lax.ppermute(value, ALONG_X, pairs)  10.6 us
    all_gather x1, blocking collectives, compute(): far_both = lax.all_gather(far_half, CORE, axis=0)  8.68 us
    ppermute x3, starting transfers between devices, shifted(): lax.ppermute(value, axis, [(source, source + steps) for source in range(c...  8.16 us
    ppermute x3, waiting for transfers between devices, shifted(): lax.ppermute(value, axis, [(source, source + steps) for source in range(c...  7.83 us
    pallas_call x3, Pallas kernels, product(): pl.pallas_call(kernel, out_shape=jax.ShapeDtypeStruct(tiles, dtype), in_s...  7.63 us
    all_gather x1, blocking collectives, compute(): lax.all_gather(jnp.concatenate([near_half, half_kv], axis=0), CORE, axis=0)  7.63 us
  transfers between devices with their start and end apart: 9, of which 5 were waited for; matrix products, arithmetic and copies ran while one was open for 2% of the time, Pallas kernels for 4%

profile of v2, /device:TPU:3, one launch (start us, length us, event | category | flops | bytes accessed | tf_op | source)
XLA Modules:
  0.0 126.2 jit_solution(4090903831569268523)
XLA Ops:
  0.6 0.0 copy-start
  0.6 1.6 %copy-done = bf16[128,8192]{1,0:T(8,128)(2,1)S(1)} copy-done((bf16[128,8192]{1,0:T(8,128)(2,1)S(1)}, bf16[128,8192]{1,0:T(8,128)(2,1)}, u32[]{:S(2)}) %copy-start) | copy-done | bytes 2097176
  2.2 0.0 copy-start.2
  2.2 0.0 copy-start.3
  2.2 0.0 copy-start.4
  2.2 0.0 copy-start.5
  2.2 0.0 copy-start.6
  2.2 0.8 shard_map.111.mine_ref
  3.1 2.6 %collective-permute-start = (bf16[4,128,2048]{2,1,0:T(8,128)(2,1)S(1)}, bf16[4,128,2048]{2,1,0:T(8,128)(2,1)}, u32[]{:S(2)}, u32[]{:S(2)}) collective-permute-start(bf16[4,128,2048]{2,1,0:T(8,128)(2,1)S(1)} %shard_map.111.mine_ref), channel_id=1, source_target_pairs={{0,1},{1,0},{2,3},{3,2},{4,5},{5,4},{6,7},{7,6},{8,9},{9,8},{10,11... | collective-permute-start | bytes 6291464 | tf_op jit(solution)/shard_map/ppermute | solution.py:278
  6.4 0.0 copy-done.2
  6.4 0.0 copy-done.3
  6.4 0.0 copy-done.4
  6.5 0.0 copy-done.5
  6.5 0.6 fusion.5
  7.1 31.8 %all_to_all.10 = bf16[32,8,128]{2,1,0:T(8,128)(2,1)S(1)} all-to-all(bf16[32,8,128]{2,1,0:T(8,128)(2,1)S(1)} %bitcast.23), channel_id=1, replica_groups=mesh['x_lo'=2,'z'=16,'y'=8,'x_hi'=2,'core'=2] {'z','core'}, dimensions={0} | all-to-all | bytes 131072 | tf_op jit(solution)/shard_map/all_to_all | solution.py:266
  39.0 0.9 broadcast_in_dim.28
  39.8 6.8 %all-to-all-start.1 = ((bf16[8,256,128]{2,1,0:T(8,128)(2,1)}), bf16[8,256,128]{2,1,0:T(8,128)(2,1)S(1)}, u32[]{:S(2)}, u32[]{:S(2)}) async-start(bf16[8,256,128]{2,1,0:T(8,128)(2,1)} %broadcast_in_dim.28), calls=%async_computation.1 | async-start | bytes 1048576 | tf_op jit(solution)/shard_map/all_to_all | solution.py:31
  46.6 0.0 copy-done.6
  46.6 3.3 %all-gather.2 = s32[2,1,128]{2,1,0:T(1,128)S(1)} all-gather(s32[1,1,128]{2,1,0:T(1,128)S(1)} %bitcast.24), channel_id=1, replica_groups=mesh['x_lo'=2,'z'=16,'y'=8,'x_hi'=2,'core'=2] {'core'}, dimensions={0}, use_global_device_ids=true | all-gather | bytes 1536 | tf_op jit(solution)/shard_map/all_gather | solution.py:279
  50.0 12.6 %all-to-all-done.1 = bf16[8,256,128]{2,1,0:T(8,128)(2,1)S(1)} async-done(((bf16[8,256,128]{2,1,0:T(8,128)(2,1)}), bf16[8,256,128]{2,1,0:T(8,128)(2,1)S(1)}, u32[]{:S(2)}, u32[]{:S(2)}) %all-to-all-start.1) | async-done | bytes 524320 | tf_op jit(solution)/shard_map/all_to_all | solution.py:31
  62.6 3.1 %collective-permute-start.1 = (bf16[2048,128]{1,0:T(8,128)(2,1)S(1)}, bf16[2048,128]{1,0:T(8,128)(2,1)S(1)}, u32[]{:S(2)}, u32[]{:S(2)}) collective-permute-start(bf16[2048,128]{1,0:T(8,128)(2,1)S(1)} %bitcast.17), channel_id=1, source_target_pairs={{0,512},{2,514},{512,2},{514,0},{1,513},{3,515},{513,3},{515,1},{4... | collective-permute-start | bytes 1572872 | tf_op jit(solution)/shard_map/ppermute | solution.py:258
  65.7 2.2 %collective-permute-start.2 = (bf16[2048,128]{1,0:T(8,128)(2,1)S(1)}, bf16[2048,128]{1,0:T(8,128)(2,1)S(1)}, u32[]{:S(2)}, u32[]{:S(2)}) collective-permute-start(bf16[2048,128]{1,0:T(8,128)(2,1)S(1)} %bitcast.18), channel_id=1, source_target_pairs={{0,514},{2,512},{512,0},{514,2},{1,515},{3,513},{513,1},{515,3},{4... | collective-permute-start | bytes 1572872 | tf_op jit(solution)/shard_map/ppermute | solution.py:258
  67.9 0.5 fusion
  68.4 7.0 %collective-permute-done.1.left_ref = bf16[2048,128]{1,0:T(8,128)(2,1)S(1)} collective-permute-done((bf16[2048,128]{1,0:T(8,128)(2,1)S(1)}, bf16[2048,128]{1,0:T(8,128)(2,1)S(1)}, u32[]{:S(2)}, u32[]{:S(2)}) %collective-permute-start.1) | collective-permute-done | bytes 524320 | tf_op jit(solution)/shard_map/ppermute | solution.py:258
  75.5 3.1 %collective-permute-start.3 = (bf16[1024,128]{1,0:T(8,128)(2,1)S(1)}, bf16[1024,128]{1,0:T(8,128)(2,1)S(1)}, u32[]{:S(2)}, u32[]{:S(2)}) collective-permute-start(bf16[1024,128]{1,0:T(8,128)(2,1)S(1)} %slice.28), channel_id=1, source_target_pairs={{0,512},{2,514},{512,2},{514,0},{1,513},{3,515},{513,3},{515,1},{4... | collective-permute-start | bytes 786440 | tf_op jit(solution)/shard_map/ppermute | solution.py:258
  78.6 0.0 collective-permute-done.2.right_ref
  78.6 2.2 %collective-permute-start.4 = (bf16[1024,128]{1,0:T(8,128)(2,1)S(1)}, bf16[1024,128]{1,0:T(8,128)(2,1)S(1)}, u32[]{:S(2)}, u32[]{:S(2)}) collective-permute-start(bf16[1024,128]{1,0:T(8,128)(2,1)S(1)} %slice.29), channel_id=1, source_target_pairs={{0,514},{2,512},{512,0},{514,2},{1,515},{3,513},{513,1},{515,3},{4... | collective-permute-start | bytes 786440 | tf_op jit(solution)/shard_map/ppermute | solution.py:258
  80.8 0.1 pad_add_fusion.place_ref
  80.9 0.1 maximum_select_fusion
  81.0 0.0 collective-permute-done.theirs_ref
  81.1 2.1 %shard_map.112.so_far_ref = f32[256,128]{1,0:T(8,128)S(1)} custom-call(s32[2]{0:T(128)S(1)} %pad_add_fusion.place_ref, bf16[4,128,2048]{2,1,0:T(8,128)(2,1)} %collective-permute-done.theirs_ref, bf16[4,128,2048]{2,1,0:T(8,128)(2,1)S(1)} %shard_map.111.mine_ref, bf16[2048,128]{1,0:T(8,128)(2,1)S(1)} %bitcast.19), custom_call_target="tpu_custom_call" | custom-call | flops 134217728 | bytes 1572864 | tf_op jit(solution)/shard_map/pallas_call | solution.py:141
  83.1 3.4 %shard_map.113.so_far_ref = f32[256,128]{1,0:T(8,128)S(1)} custom-call(s32[2]{0:T(128)S(1)} %pad_add_fusion.place_ref, bf16[4,128,2048]{2,1,0:T(8,128)(2,1)} %collective-permute-done.theirs_ref, bf16[4,128,2048]{2,1,0:T(8,128)(2,1)S(1)} %shard_map.111.mine_ref, f32[256,128]{1,0:T(8,128)S(1)} %shard_map.112.so_far_ref, ...), custom_call_target="tpu_custom_call" | custom-call | flops 268435456 | bytes 3145728 | tf_op jit(solution)/shard_map/pallas_call | solution.py:141
  86.6 0.0 collective-permute-done.3.low_ref
  86.6 0.0 collective-permute-done.4.high_ref
  86.6 0.0 copy-start.1
  86.6 2.1 %shard_map.114 = bf16[256,128]{1,0:T(8,128)(2,1)S(1)} custom-call(s32[2]{0:T(128)S(1)} %pad_add_fusion.place_ref, bf16[4,128,2048]{2,1,0:T(8,128)(2,1)} %collective-permute-done.theirs_ref, bf16[4,128,2048]{2,1,0:T(8,128)(2,1)S(1)} %shard_map.111.mine_ref, f32[256,128]{1,0:T(8,128)S(1)} %shard_map.113.so_far_ref, ...), custom_call_target="tpu_custom_call" | custom-call | flops 134217728 | bytes 1572864 | tf_op jit(solution)/shard_map/pallas_call | solution.py:141
  88.7 4.3 %collective-permute-start.6 = (bf16[256,128]{1,0:T(8,128)(2,1)S(1)}, bf16[256,128]{1,0:T(8,128)(2,1)S(1)}, u32[]{:S(2)}, u32[]{:S(2)}) collective-permute-start(bf16[256,128]{1,0:T(8,128)(2,1)S(1)} %shard_map.114), channel_id=1, source_target_pairs={{0,2},{2,4},{4,6},{6,8},{8,10},{10,12},{12,14},{14,16},{16,18},{18... | collective-permute-start | bytes 196616 | tf_op jit(solution)/shard_map/ppermute | solution.py:249
  93.1 1.9 %collective-permute-start.5 = (bf16[256,128]{1,0:T(8,128)(2,1)S(1)}, bf16[256,128]{1,0:T(8,128)(2,1)S(1)}, u32[]{:S(2)}, u32[]{:S(2)}) collective-permute-start(bf16[256,128]{1,0:T(8,128)(2,1)S(1)} %shard_map.114), channel_id=1, source_target_pairs={{0,4},{2,6},{4,8},{6,10},{8,12},{10,14},{12,16},{14,18},{16,20},{1... | collective-permute-start | bytes 196616 | tf_op jit(solution)/shard_map/ppermute | solution.py:249
  95.0 0.1 pad_maximum_fusion.2
  95.1 2.9 %collective-permute-done.6 = bf16[256,128]{1,0:T(8,128)(2,1)S(1)} collective-permute-done((bf16[256,128]{1,0:T(8,128)(2,1)S(1)}, bf16[256,128]{1,0:T(8,128)(2,1)S(1)}, u32[]{:S(2)}, u32[]{:S(2)}) %collective-permute-start.6) | collective-permute-done | bytes 65568 | tf_op jit(solution)/shard_map/ppermute | solution.py:249
  98.0 4.6 %collective-permute-done.5 = bf16[256,128]{1,0:T(8,128)(2,1)S(1)} collective-permute-done((bf16[256,128]{1,0:T(8,128)(2,1)S(1)}, bf16[256,128]{1,0:T(8,128)(2,1)S(1)}, u32[]{:S(2)}, u32[]{:S(2)}) %collective-permute-start.5) | collective-permute-done | bytes 65568 | tf_op jit(solution)/shard_map/ppermute | solution.py:249
  102.6 1.9 %collective-permute-start.7 = (bf16[512,128]{1,0:T(8,128)(2,1)S(1)}, bf16[512,128]{1,0:T(8,128)(2,1)S(1)}, u32[]{:S(2)}, u32[]{:S(2)}) collective-permute-start(bf16[512,128]{1,0:T(8,128)(2,1)S(1)} %pad_maximum_fusion.1), channel_id=1, source_target_pairs={{0,4},{2,6},{4,8},{6,10},{8,12},{10,14},{12,16},{14,18},{16,20},{1... | collective-permute-start | bytes 393224 | tf_op jit(solution)/shard_map/ppermute | solution.py:249
  104.6 7.6 %all-gather.1 = bf16[1536,128]{1,0:T(8,128)(2,1)S(1)} all-gather(bf16[768,128]{1,0:T(8,128)(2,1)S(1)} %pad_maximum_fusion), channel_id=3, replica_groups=mesh['x_lo'=2,'z'=16,'y'=8,'x_hi'=2,'core'=2] {'core'}, dimensions={0}, use_global_device_ids=true | all-gather | bytes 589824 | tf_op jit(solution)/shard_map/all_gather | solution.py:307
  112.2 0.3 collective-permute-done.7
  112.5 8.7 %all-gather = bf16[1024,128]{1,0:T(8,128)(2,1)S(1)} all-gather(bf16[512,128]{1,0:T(8,128)(2,1)S(1)} %collective-permute-done.7), channel_id=2, replica_groups=mesh['x_lo'=2,'z'=16,'y'=8,'x_hi'=2,'core'=2] {'core'}, dimensions={0}, use_global_device_ids=true | all-gather | bytes 393216 | tf_op jit(solution)/shard_map/all_gather | solution.py:310
  121.2 0.1 broadcast_in_dim.31.first_ref
  121.3 0.0 copy-done.1
  121.3 4.9 %shard_map.115 = bf16[128,1024]{1,0:T(8,128)(2,1)} custom-call(s32[1]{0:T(128)} %bitcast.offset_ref, bf16[2,512,128]{2,1,0:T(8,128)(2,1)S(1)} %bitcast.21, bf16[2,768,128]{2,1,0:T(8,128)(2,1)S(1)} %bitcast.20, bf16[128,1024]{1,0:T(8,128)(2,1)S(1)} %copy-done.1, s32[128,128]{1,0:T(8,128)S(1)} %broadcast_in_dim.31.first_ref, ...), custom_call_target="tpu_custom_call" | custom-call | flops 603979776 | bytes 1179648 | tf_op jit(solution)/shard_map/pallas_call | solution.py:218
  (10 shorter events, 0.1 us)
Async XLA Ops:
  0.6 1.6 %copy-start = (bf16[128,8192]{1,0:T(8,128)(2,1)S(1)}, bf16[128,8192]{1,0:T(8,128)(2,1)}, u32[]{:S(2)}) copy-start(bf16[128,8192]{1,0:T(8,128)(2,1)} %tokens_ref.1) | copy-start | bytes 6291460
  2.2 4.2 %copy-start.2 = (f32[8,256]{1,0:T(8,128)S(1)}, f32[8,256]{1,0:T(8,128)}, u32[]{:S(2)}) copy-start(f32[8,256]{1,0:T(8,128)} %param.12) | copy-start | bytes 24580
  2.2 4.2 %copy-start.3 = (f32[8,256]{1,0:T(8,128)S(1)}, f32[8,256]{1,0:T(8,128)}, u32[]{:S(2)}) copy-start(f32[8,256]{1,0:T(8,128)} %param.11) | copy-start | bytes 24580
  2.2 4.2 %copy-start.4 = (f32[8,256]{1,0:T(8,128)S(1)}, f32[8,256]{1,0:T(8,128)}, u32[]{:S(2)}) copy-start(f32[8,256]{1,0:T(8,128)} %param.13) | copy-start | bytes 24580
  2.2 4.2 %copy-start.5 = (f32[8,256]{1,0:T(8,128)S(1)}, f32[8,256]{1,0:T(8,128)}, u32[]{:S(2)}) copy-start(f32[8,256]{1,0:T(8,128)} %param.14) | copy-start | bytes 24580
  2.2 44.4 %copy-start.6 = (s32[128]{0:T(128)S(1)}, s32[128]{0:T(128)}, u32[]{:S(2)}) copy-start(s32[128]{0:T(128)} %param.10) | copy-start | bytes 1540
  3.1 77.9 %collective-permute-start = (bf16[4,128,2048]{2,1,0:T(8,128)(2,1)S(1)}, bf16[4,128,2048]{2,1,0:T(8,128)(2,1)}, u32[]{:S(2)}, u32[]{:S(2)}) collective-permute-start(bf16[4,128,2048]{2,1,0:T(8,128)(2,1)S(1)} %shard_map.111.mine_ref), channel_id=1, source_target_pairs={{0,1},{1,0},{2,3},{3,2},{4,5},{5,4},{6,7},{7,6},{8,9},{9,8},{10,11... | collective-permute-start | bytes 6291464 | tf_op jit(solution)/shard_map/ppermute | solution.py:278
  39.8 22.8 %all-to-all-start.1 = ((bf16[8,256,128]{2,1,0:T(8,128)(2,1)}), bf16[8,256,128]{2,1,0:T(8,128)(2,1)S(1)}, u32[]{:S(2)}, u32[]{:S(2)}) async-start(bf16[8,256,128]{2,1,0:T(8,128)(2,1)} %broadcast_in_dim.28), calls=%async_computation.1 | async-start | bytes 1048576 | tf_op jit(solution)/shard_map/all_to_all | solution.py:31
  62.6 12.9 %collective-permute-start.1 = (bf16[2048,128]{1,0:T(8,128)(2,1)S(1)}, bf16[2048,128]{1,0:T(8,128)(2,1)S(1)}, u32[]{:S(2)}, u32[]{:S(2)}) collective-permute-start(bf16[2048,128]{1,0:T(8,128)(2,1)S(1)} %bitcast.17), channel_id=1, source_target_pairs={{0,512},{2,514},{512,2},{514,0},{1,513},{3,515},{513,3},{515,1},{4... | collective-permute-start | bytes 1572872 | tf_op jit(solution)/shard_map/ppermute | solution.py:258
  65.7 12.9 %collective-permute-start.2 = (bf16[2048,128]{1,0:T(8,128)(2,1)S(1)}, bf16[2048,128]{1,0:T(8,128)(2,1)S(1)}, u32[]{:S(2)}, u32[]{:S(2)}) collective-permute-start(bf16[2048,128]{1,0:T(8,128)(2,1)S(1)} %bitcast.18), channel_id=1, source_target_pairs={{0,514},{2,512},{512,0},{514,2},{1,515},{3,513},{513,1},{515,3},{4... | collective-permute-start | bytes 1572872 | tf_op jit(solution)/shard_map/ppermute | solution.py:258
  75.5 11.1 %collective-permute-start.3 = (bf16[1024,128]{1,0:T(8,128)(2,1)S(1)}, bf16[1024,128]{1,0:T(8,128)(2,1)S(1)}, u32[]{:S(2)}, u32[]{:S(2)}) collective-permute-start(bf16[1024,128]{1,0:T(8,128)(2,1)S(1)} %slice.28), channel_id=1, source_target_pairs={{0,512},{2,514},{512,2},{514,0},{1,513},{3,515},{513,3},{515,1},{4... | collective-permute-start | bytes 786440 | tf_op jit(solution)/shard_map/ppermute | solution.py:258
  78.6 7.9 %collective-permute-start.4 = (bf16[1024,128]{1,0:T(8,128)(2,1)S(1)}, bf16[1024,128]{1,0:T(8,128)(2,1)S(1)}, u32[]{:S(2)}, u32[]{:S(2)}) collective-permute-start(bf16[1024,128]{1,0:T(8,128)(2,1)S(1)} %slice.29), channel_id=1, source_target_pairs={{0,514},{2,512},{512,0},{514,2},{1,515},{3,513},{513,1},{515,3},{4... | collective-permute-start | bytes 786440 | tf_op jit(solution)/shard_map/ppermute | solution.py:258
  86.6 34.7 %copy-start.1 = (bf16[128,1024]{1,0:T(8,128)(2,1)S(1)}, bf16[128,1024]{1,0:T(8,128)(2,1)}, u32[]{:S(2)}) copy-start(bf16[128,1024]{1,0:T(8,128)(2,1)} %queries_ref.1) | copy-start | bytes 786436
  88.7 9.2 %collective-permute-start.6 = (bf16[256,128]{1,0:T(8,128)(2,1)S(1)}, bf16[256,128]{1,0:T(8,128)(2,1)S(1)}, u32[]{:S(2)}, u32[]{:S(2)}) collective-permute-start(bf16[256,128]{1,0:T(8,128)(2,1)S(1)} %shard_map.114), channel_id=1, source_target_pairs={{0,2},{2,4},{4,6},{6,8},{8,10},{10,12},{12,14},{14,16},{16,18},{18... | collective-permute-start | bytes 196616 | tf_op jit(solution)/shard_map/ppermute | solution.py:249
  93.1 9.5 %collective-permute-start.5 = (bf16[256,128]{1,0:T(8,128)(2,1)S(1)}, bf16[256,128]{1,0:T(8,128)(2,1)S(1)}, u32[]{:S(2)}, u32[]{:S(2)}) collective-permute-start(bf16[256,128]{1,0:T(8,128)(2,1)S(1)} %shard_map.114), channel_id=1, source_target_pairs={{0,4},{2,6},{4,8},{6,10},{8,12},{10,14},{12,16},{14,18},{16,20},{1... | collective-permute-start | bytes 196616 | tf_op jit(solution)/shard_map/ppermute | solution.py:249
  102.6 9.9 %collective-permute-start.7 = (bf16[512,128]{1,0:T(8,128)(2,1)S(1)}, bf16[512,128]{1,0:T(8,128)(2,1)S(1)}, u32[]{:S(2)}, u32[]{:S(2)}) collective-permute-start(bf16[512,128]{1,0:T(8,128)(2,1)S(1)} %pad_maximum_fusion.1), channel_id=1, source_target_pairs={{0,4},{2,6},{4,8},{6,10},{8,12},{10,14},{12,16},{14,18},{16,20},{1... | collective-permute-start | bytes 393224 | tf_op jit(solution)/shard_map/ppermute | solution.py:249

commit v3 on v2

--- a/solution.py
+++ b/solution.py
@@ -87,9 +87,13 @@
     )(tokens)
 
 
-def plane_product(mine_ref, theirs_ref, plane, pieces, columns, held, arrival):
+def plane_fetch(theirs_ref, plane, held, arrival):
     fetch = pltpu.make_async_copy(theirs_ref.at[plane], held, arrival)
     fetch.start()
+    return fetch
+
+
+def plane_product(mine_ref, plane, pieces, columns, held, fetch):
     depth, along_y = 16, 8 // len(pieces)
     for order, piece_ref in enumerate(pieces):
         for y in range(along_y):
@@ -105,18 +109,21 @@
 
 
 def own_kernel(place_ref, theirs_ref, mine_ref, piece_ref, out_ref, columns, held, arrival):
-    out_ref[...] = plane_product(
-        mine_ref, theirs_ref, place_ref[1], (piece_ref,), columns, held, arrival
-    )
+    plane = place_ref[1]
+    fetch = plane_fetch(theirs_ref, plane, held, arrival)
+    out_ref[...] = plane_product(mine_ref, plane, (piece_ref,), columns, held, fetch)
 
 
 def beside_kernel(
-    place_ref, theirs_ref, mine_ref, so_far_ref, left_ref, right_ref, out_ref, *scratches
+    place_ref, theirs_ref, mine_ref, so_far_ref, left_ref, right_ref, out_ref,
+    columns, more, held, also, arrival, later,
 ):
     left = (place_ref[1] + 3) & 3
     right = (place_ref[1] + 1) & 3
-    from_left = plane_product(mine_ref, theirs_ref, left, (left_ref,), *scratches[0::2])
-    from_right = plane_product(mine_ref, theirs_ref, right, (right_ref,), *scratches[1::2])
+    fetch = plane_fetch(theirs_ref, left, held, arrival)
+    other_fetch = plane_fetch(theirs_ref, right, also, later)
+    from_left = plane_product(mine_ref, left, (left_ref,), columns, held, fetch)
+    from_right = plane_product(mine_ref, right, (right_ref,), more, also, other_fetch)
     out_ref[...] = so_far_ref[...] + from_left + from_right
 
 
@@ -126,8 +133,9 @@
 ):
     across = (place_ref[1] + 2) & 3
     core = place_ref[0]
+    fetch = plane_fetch(theirs_ref, across, held, arrival)
     total = so_far_ref[...] + plane_product(
-        mine_ref, theirs_ref, across, (low_ref, high_ref), columns, held, arrival
+        mine_ref, across, (low_ref, high_ref), columns, held, fetch
     )
     count = mine_ref.shape[1]
     done = turned(total, cosine_ref[...], sine_ref[...]).astype(jnp.bfloat16)
@@ -171,46 +179,54 @@
     count, width = queries_ref.shape
     head_dim = cosine_ref.shape[1]
     held = far_ref.shape[1]
-    seen = windows[0].shape[0] - count
-    reach = seen - count
+    reach = held
+    seen = reach + count
     near = pl.ds(pl.multiple_of(offset_ref[0], 128), seen)
     for kind, window in enumerate(windows):
         window[:held] = far_ref[kind]
         window[held:] = near_ref[kind]
     keys, values = (window[near] for window in windows)
-    row = lax.broadcasted_iota(jnp.int32, (count, head_dim), 0)
-    column = lax.broadcasted_iota(jnp.int32, (count, head_dim), 1)
-    first = first_ref[...]
-    bias = jnp.concatenate(
-        [
-            jnp.where(
-                (column + (start - reach) <= row) & (column + (start - reach) >= first),
-                0.0,
-                masked_score,
-            )
-            for start in range(0, seen, head_dim)
-        ],
-        axis=1,
-    )
+    token = lax.broadcasted_iota(jnp.int32, (seen, count), 0) - reach
+    query = lax.broadcasted_iota(jnp.int32, (seen, count), 1)
+    allowed = (token <= query) & (token >= first_ref[0:1, :])
+    bias = jnp.where(allowed, 0.0, masked_score).astype(jnp.bfloat16)
+    keys = jnp.concatenate([keys, bias], axis=1)
+    row = lax.broadcasted_iota(jnp.int32, (count, count), 0)
+    column = lax.broadcasted_iota(jnp.int32, (count, count), 1)
+    unit = (row == column).astype(jnp.float32).astype(jnp.bfloat16)
     cosine, sine = cosine_ref[...], sine_ref[...]
     scale = head_dim**-0.5 * math.log2(math.e)
-    for head in range(width // head_dim):
-        lanes = slice(head * head_dim, (head + 1) * head_dim)
-        rows = turned(queries_ref[:, lanes].astype(jnp.float32), cosine, sine)
+    heads = width // head_dim
+    for start in range(0, heads, 4):
+        rows = jnp.concatenate(
+            [
+                jnp.concatenate(
+                    [
+                        turned(
+                            queries_ref[:, h * head_dim : (h + 1) * head_dim].astype(jnp.float32),
+                            cosine,
+                            sine,
+                        ).astype(jnp.bfloat16),
+                        unit,
+                    ],
+                    axis=1,
+                )
+                for h in range(start, start + 4)
+            ],
+            axis=0,
+        )
         scores = lax.dot_general(
-            rows.astype(jnp.bfloat16),
-            keys,
-            (((1,), (1,)), ((), ())),
-            preferred_element_type=jnp.float32,
+            rows, keys, (((1,), (1,)), ((), ())), preferred_element_type=jnp.float32
         )
-        scores = scores + bias
         top_score = jnp.max(scores, axis=1, keepdims=True)
         weights = jnp.exp2((scores - top_score) * scale)
         share = 1.0 / jnp.sum(weights, axis=1, keepdims=True)
         probs = (weights * share).astype(jnp.bfloat16)
-        out_ref[:, lanes] = jnp.dot(
-            probs, values, preferred_element_type=jnp.float32
-        ).astype(jnp.bfloat16)
+        result = jnp.dot(probs, values, preferred_element_type=jnp.float32).astype(jnp.bfloat16)
+        for h in range(4):
+            out_ref[:, (start + h) * head_dim : (start + h + 1) * head_dim] = result[
+                h * count : (h + 1) * count
+            ]
 
 
 def attend(offset, far, close, queries, first, cosine, sine):
@@ -223,7 +239,7 @@
         scratch_shapes=[pltpu.VMEM((far.shape[1] + close.shape[1], close.shape[2]), jnp.bfloat16)] * 2,
         compiler_params=room(20),
         cost_estimate=pl.CostEstimate(
-            flops=4 * count * width * 1152,
+            flops=6 * count * width * 1152,
             bytes_accessed=4 * count * width + 2 * far.size + 2 * close.size,
             transcendentals=count * width * 9,
         ),
@@ -284,8 +300,7 @@
     key_cosine = jnp.where(is_keys, jnp.concatenate([cosine, cosine_other]), 1.0)
     key_sine = jnp.where(is_keys, jnp.concatenate([sine, sine_other]), 0.0)
     first = jnp.broadcast_to(
-        (jnp.arange(local_count, dtype=jnp.int32) - positions)[:, None],
-        (local_count, head_dim),
+        (jnp.arange(local_count, dtype=jnp.int32) - positions)[None, :], (8, local_count)
     )
     over_y = from_everyone(over_z, ALONG_Y).reshape(-1, head_dim)
     half = over_y.shape[0] // 2
@@ -300,15 +315,12 @@
         across_kernel, place, theirs, mine, tiles, jnp.bfloat16, 1,
         so_far, across_low, across_high, key_cosine, key_sine,
     )
-    one_back = shifted(half_kv, CHIPS, 1)
-    two_back = shifted(half_kv, CHIPS, 2)
-    near_half = jnp.concatenate([two_back, one_back], axis=0)
-    far_half = shifted(near_half, CHIPS, 2)
-    near_both = lax.all_gather(
-        jnp.concatenate([near_half, half_kv], axis=0), CORE, axis=0
-    )
-    far_both = lax.all_gather(far_half, CORE, axis=0)
-    offset = core * local_count
+    row_kv = lax.all_gather(half_kv, X_HI, axis=0, tiled=True)
+    one_back = shifted(row_kv, CHIPS, 2)
+    two_back = shifted(row_kv, CHIPS, 4)
+    near_both = lax.all_gather(row_kv, CORE, axis=0)
+    far_both = lax.all_gather(jnp.concatenate([two_back, one_back], axis=0), CORE, axis=0)
+    offset = lax.axis_index(("x_hi", "core")) * local_count
     attention = attend(
         offset.astype(jnp.int32)[None], far_both, near_both, queries, first, cosine, sine
     )

time: 127 us -> 121 us (0.953)
  the two profiles are of different devices: /device:TPU:3 before, /device:TPU:6 now
where the time goes in v3:
time: 121 us; the launch traced here: 120 us
  blocking collectives  46 us (38%)
  waiting for transfers between devices  32.6 us (27%)
  starting transfers between devices  25 us (21%)
  Pallas kernels  11 us (9%)
  local copies, waits for them, and re-layouts  2.52 us (2%)
  between operations  1.6 us (1%)
  other arithmetic  1.52 us (1%)
    all_to_all x1, blocking collectives, column_halves(): return lax.all_to_all(copies, axes, split_axis=0, concat_axis=0, tiled=True)  33.4 us
    all_to_all x1, waiting for transfers between devices, from_everyone(): return lax.all_to_all(copies, axis, split_axis=0, concat_axis=0, tiled=True)  14.8 us
    ppermute x4, starting transfers between devices, along_x(): return lax.ppermute(value, ALONG_X, pairs)  11.7 us
    ppermute x4, waiting for transfers between devices, along_x(): return lax.ppermute(value, ALONG_X, pairs)  9.89 us
    ppermute x2, waiting for transfers between devices, shifted(): lax.ppermute(value, axis, [(source, source + steps) for source in range(c...  8 us
    all_to_all x1, starting transfers between devices, from_everyone(): return lax.all_to_all(copies, axis, split_axis=0, concat_axis=0, tiled=True)  7.1 us
    all_gather x1, blocking collectives, compute(): row_kv = lax.all_gather(half_kv, X_HI, axis=0, tiled=True)  6.57 us
    pallas_call x3, Pallas kernels, product(): pl.pallas_call(kernel, out_shape=jax.ShapeDtypeStruct(tiles, dtype), in_s...  6.53 us
  transfers between devices with their start and end apart: 8, of which 5 were waited for; matrix products, arithmetic and copies ran while one was open for 2% of the time, Pallas kernels for 4%

profile of v3, /device:TPU:6, one launch (start us, length us, event | category | flops | bytes accessed | tf_op | source)
XLA Modules:
  0.0 120.2 jit_solution(11084886278496520118)
XLA Ops:
  0.6 0.0 copy-start
  0.6 1.6 %copy-done = bf16[128,8192]{1,0:T(8,128)(2,1)S(1)} copy-done((bf16[128,8192]{1,0:T(8,128)(2,1)S(1)}, bf16[128,8192]{1,0:T(8,128)(2,1)}, u32[]{:S(2)}) %copy-start) | copy-done | bytes 2097176
  2.2 0.0 copy-start.2
  2.2 0.0 copy-start.3
  2.2 0.0 copy-start.4
  2.2 0.0 copy-start.5
  2.2 0.0 copy-start.6
  2.2 0.8 shard_map.111.mine_ref
  3.1 1.9 %collective-permute-start = (bf16[4,128,2048]{2,1,0:T(8,128)(2,1)S(1)}, bf16[4,128,2048]{2,1,0:T(8,128)(2,1)}, u32[]{:S(2)}, u32[]{:S(2)}) collective-permute-start(bf16[4,128,2048]{2,1,0:T(8,128)(2,1)S(1)} %shard_map.111.mine_ref), channel_id=1, source_target_pairs={{0,1},{1,0},{2,3},{3,2},{4,5},{5,4},{6,7},{7,6},{8,9},{9,8},{10,11... | collective-permute-start | bytes 6291464 | tf_op jit(solution)/shard_map/ppermute | solution.py:294
  5.8 0.0 copy-done.2
  5.8 0.0 copy-done.3
  5.8 0.0 copy-done.4
  5.8 0.0 copy-done.5
  5.8 0.6 fusion.5
  6.5 33.4 %all_to_all.10 = bf16[32,8,128]{2,1,0:T(8,128)(2,1)S(1)} all-to-all(bf16[32,8,128]{2,1,0:T(8,128)(2,1)S(1)} %bitcast.23), channel_id=1, replica_groups=mesh['x_lo'=2,'z'=16,'y'=8,'x_hi'=2,'core'=2] {'z','core'}, dimensions={0} | all-to-all | bytes 131072 | tf_op jit(solution)/shard_map/all_to_all | solution.py:282
  39.9 0.9 broadcast_in_dim.28
  40.7 7.1 %all-to-all-start.1 = ((bf16[8,256,128]{2,1,0:T(8,128)(2,1)}), bf16[8,256,128]{2,1,0:T(8,128)(2,1)S(1)}, u32[]{:S(2)}, u32[]{:S(2)}) async-start(bf16[8,256,128]{2,1,0:T(8,128)(2,1)} %broadcast_in_dim.28), calls=%async_computation.1 | async-start | bytes 1048576 | tf_op jit(solution)/shard_map/all_to_all | solution.py:31
  47.8 0.0 copy-done.6
  47.8 1.8 %all-gather.2 = s32[2,1,128]{2,1,0:T(1,128)S(1)} all-gather(s32[1,1,128]{2,1,0:T(1,128)S(1)} %bitcast.24), channel_id=1, replica_groups=mesh['x_lo'=2,'z'=16,'y'=8,'x_hi'=2,'core'=2] {'core'}, dimensions={0}, use_global_device_ids=true | all-gather | bytes 1536 | tf_op jit(solution)/shard_map/all_gather | solution.py:295
  49.7 14.8 %all-to-all-done.1 = bf16[8,256,128]{2,1,0:T(8,128)(2,1)S(1)} async-done(((bf16[8,256,128]{2,1,0:T(8,128)(2,1)}), bf16[8,256,128]{2,1,0:T(8,128)(2,1)S(1)}, u32[]{:S(2)}, u32[]{:S(2)}) %all-to-all-start.1) | async-done | bytes 524320 | tf_op jit(solution)/shard_map/all_to_all | solution.py:31
  64.4 2.4 %collective-permute-start.1 = (bf16[2048,128]{1,0:T(8,128)(2,1)S(1)}, bf16[2048,128]{1,0:T(8,128)(2,1)S(1)}, u32[]{:S(2)}, u32[]{:S(2)}) collective-permute-start(bf16[2048,128]{1,0:T(8,128)(2,1)S(1)} %bitcast.17), channel_id=1, source_target_pairs={{0,512},{2,514},{512,2},{514,0},{1,513},{3,515},{513,3},{515,1},{4... | collective-permute-start | bytes 1572872 | tf_op jit(solution)/shard_map/ppermute | solution.py:274
  66.8 3.5 %collective-permute-start.2 = (bf16[2048,128]{1,0:T(8,128)(2,1)S(1)}, bf16[2048,128]{1,0:T(8,128)(2,1)S(1)}, u32[]{:S(2)}, u32[]{:S(2)}) collective-permute-start(bf16[2048,128]{1,0:T(8,128)(2,1)S(1)} %bitcast.18), channel_id=1, source_target_pairs={{0,514},{2,512},{512,0},{514,2},{1,515},{3,513},{513,1},{515,3},{4... | collective-permute-start | bytes 1572872 | tf_op jit(solution)/shard_map/ppermute | solution.py:274
  70.3 0.5 fusion
  70.8 7.3 %collective-permute-done.1.left_ref = bf16[2048,128]{1,0:T(8,128)(2,1)S(1)} collective-permute-done((bf16[2048,128]{1,0:T(8,128)(2,1)S(1)}, bf16[2048,128]{1,0:T(8,128)(2,1)S(1)}, u32[]{:S(2)}, u32[]{:S(2)}) %collective-permute-start.1) | collective-permute-done | bytes 524320 | tf_op jit(solution)/shard_map/ppermute | solution.py:274
  78.2 3.6 %collective-permute-start.3 = (bf16[1024,128]{1,0:T(8,128)(2,1)S(1)}, bf16[1024,128]{1,0:T(8,128)(2,1)S(1)}, u32[]{:S(2)}, u32[]{:S(2)}) collective-permute-start(bf16[1024,128]{1,0:T(8,128)(2,1)S(1)} %slice.28), channel_id=1, source_target_pairs={{0,512},{2,514},{512,2},{514,0},{1,513},{3,515},{513,3},{515,1},{4... | collective-permute-start | bytes 786440 | tf_op jit(solution)/shard_map/ppermute | solution.py:274
  81.8 0.0 collective-permute-done.2.right_ref
  81.8 2.2 %collective-permute-start.4 = (bf16[1024,128]{1,0:T(8,128)(2,1)S(1)}, bf16[1024,128]{1,0:T(8,128)(2,1)S(1)}, u32[]{:S(2)}, u32[]{:S(2)}) collective-permute-start(bf16[1024,128]{1,0:T(8,128)(2,1)S(1)} %slice.29), channel_id=1, source_target_pairs={{0,514},{2,512},{512,0},{514,2},{1,515},{3,513},{513,1},{515,3},{4... | collective-permute-start | bytes 786440 | tf_op jit(solution)/shard_map/ppermute | solution.py:274
  84.1 0.1 pad_add_fusion.place_ref
  84.1 0.1 maximum_select_fusion
  84.3 0.0 collective-permute-done.theirs_ref
  84.3 2.1 %shard_map.112.so_far_ref = f32[256,128]{1,0:T(8,128)S(1)} custom-call(s32[2]{0:T(128)S(1)} %pad_add_fusion.place_ref, bf16[4,128,2048]{2,1,0:T(8,128)(2,1)} %collective-permute-done.theirs_ref, bf16[4,128,2048]{2,1,0:T(8,128)(2,1)S(1)} %shard_map.111.mine_ref, bf16[2048,128]{1,0:T(8,128)(2,1)S(1)} %bitcast.19), custom_call_target="tpu_custom_call" | custom-call | flops 134217728 | bytes 1572864 | tf_op jit(solution)/shard_map/pallas_call | solution.py:149
  86.4 2.3 %shard_map.113.so_far_ref = f32[256,128]{1,0:T(8,128)S(1)} custom-call(s32[2]{0:T(128)S(1)} %pad_add_fusion.place_ref, bf16[4,128,2048]{2,1,0:T(8,128)(2,1)} %collective-permute-done.theirs_ref, bf16[4,128,2048]{2,1,0:T(8,128)(2,1)S(1)} %shard_map.111.mine_ref, f32[256,128]{1,0:T(8,128)S(1)} %shard_map.112.so_far_ref, ...), custom_call_target="tpu_custom_call" | custom-call | flops 268435456 | bytes 3145728 | tf_op jit(solution)/shard_map/pallas_call | solution.py:149
  88.7 0.0 collective-permute-done.3.low_ref
  88.7 2.6 %collective-permute-done.4.high_ref = bf16[1024,128]{1,0:T(8,128)(2,1)S(1)} collective-permute-done((bf16[1024,128]{1,0:T(8,128)(2,1)S(1)}, bf16[1024,128]{1,0:T(8,128)(2,1)S(1)}, u32[]{:S(2)}, u32[]{:S(2)}) %collective-permute-start.4) | collective-permute-done | bytes 262176 | tf_op jit(solution)/shard_map/ppermute | solution.py:274
  91.3 2.1 %shard_map.114 = bf16[256,128]{1,0:T(8,128)(2,1)S(1)} custom-call(s32[2]{0:T(128)S(1)} %pad_add_fusion.place_ref, bf16[4,128,2048]{2,1,0:T(8,128)(2,1)} %collective-permute-done.theirs_ref, bf16[4,128,2048]{2,1,0:T(8,128)(2,1)S(1)} %shard_map.111.mine_ref, f32[256,128]{1,0:T(8,128)S(1)} %shard_map.113.so_far_ref, ...), custom_call_target="tpu_custom_call" | custom-call | flops 134217728 | bytes 1572864 | tf_op jit(solution)/shard_map/pallas_call | solution.py:149
  93.4 0.0 copy-start.1
  93.4 6.6 %all_gather.19 = bf16[512,128]{1,0:T(8,128)(2,1)S(1)} all-gather(bf16[256,128]{1,0:T(8,128)(2,1)S(1)} %shard_map.114), channel_id=1, replica_groups=mesh['x_lo'=2,'z'=16,'y'=8,'x_hi'=2,'core'=2] {'x_hi'}, dimensions={0}, use_global_device_ids=true | all-gather | bytes 196608 | tf_op jit(solution)/shard_map/all_gather | solution.py:318
  100.0 1.9 %collective-permute-start.6 = (bf16[512,128]{1,0:T(8,128)(2,1)S(1)}, bf16[512,128]{1,0:T(8,128)(2,1)S(1)}, u32[]{:S(2)}, u32[]{:S(2)}) collective-permute-start(bf16[512,128]{1,0:T(8,128)(2,1)S(1)} %all_gather.19), channel_id=1, source_target_pairs={{0,4},{2,6},{4,8},{6,10},{8,12},{10,14},{12,16},{14,18},{16,20},{1... | collective-permute-start | bytes 393224 | tf_op jit(solution)/shard_map/ppermute | solution.py:265
  101.9 2.4 %collective-permute-start.5 = (bf16[512,128]{1,0:T(8,128)(2,1)S(1)}, bf16[512,128]{1,0:T(8,128)(2,1)S(1)}, u32[]{:S(2)}, u32[]{:S(2)}) collective-permute-start(bf16[512,128]{1,0:T(8,128)(2,1)S(1)} %all_gather.19), channel_id=1, source_target_pairs={{0,8},{2,10},{4,12},{6,14},{8,16},{10,18},{12,20},{14,22},{16,24},... | collective-permute-start | bytes 393224 | tf_op jit(solution)/shard_map/ppermute | solution.py:265
  104.3 0.1 pad_maximum_fusion.1
  104.4 2.0 %all-gather.1 = bf16[1024,128]{1,0:T(8,128)(2,1)S(1)} all-gather(bf16[512,128]{1,0:T(8,128)(2,1)S(1)} %all_gather.19), channel_id=3, replica_groups=mesh['x_lo'=2,'z'=16,'y'=8,'x_hi'=2,'core'=2] {'core'}, dimensions={0}, use_global_device_ids=true | all-gather | bytes 393216 | tf_op jit(solution)/shard_map/all_gather | solution.py:321
  106.4 4.7 %collective-permute-done.6 = bf16[512,128]{1,0:T(8,128)(2,1)S(1)} collective-permute-done((bf16[512,128]{1,0:T(8,128)(2,1)S(1)}, bf16[512,128]{1,0:T(8,128)(2,1)S(1)}, u32[]{:S(2)}, u32[]{:S(2)}) %collective-permute-start.6) | collective-permute-done | bytes 131104 | tf_op jit(solution)/shard_map/ppermute | solution.py:265
  111.1 3.3 %collective-permute-done.5 = bf16[512,128]{1,0:T(8,128)(2,1)S(1)} collective-permute-done((bf16[512,128]{1,0:T(8,128)(2,1)S(1)}, bf16[512,128]{1,0:T(8,128)(2,1)S(1)}, u32[]{:S(2)}, u32[]{:S(2)}) %collective-permute-start.5) | collective-permute-done | bytes 131104 | tf_op jit(solution)/shard_map/ppermute | solution.py:265
  114.4 2.2 %all-gather = bf16[2048,128]{1,0:T(8,128)(2,1)S(1)} all-gather(bf16[1024,128]{1,0:T(8,128)(2,1)S(1)} %pad_maximum_fusion), channel_id=2, replica_groups=mesh['x_lo'=2,'z'=16,'y'=8,'x_hi'=2,'core'=2] {'core'}, dimensions={0}, use_global_device_ids=true | all-gather | bytes 786432 | tf_op jit(solution)/shard_map/all_gather | solution.py:322
  116.6 0.0 copy-done.1
  116.6 3.6 %shard_map.115 = bf16[128,1024]{1,0:T(8,128)(2,1)} custom-call(s32[1]{0:T(128)} %bitcast.offset_ref, bf16[2,1024,128]{2,1,0:T(8,128)(2,1)S(1)} %bitcast.20, bf16[2,512,128]{2,1,0:T(8,128)(2,1)S(1)} %bitcast.21, bf16[128,1024]{1,0:T(8,128)(2,1)S(1)} %copy-done.1, s32[8,128]{1,0:T(8,128)S(1)} %broadcast_in_dim.31.first_ref, ...), custom_call_target="tpu_custom_call" | custom-call | flops 905969664 | bytes 1310720 | tf_op jit(solution)/shard_map/pallas_call | solution.py:234
  (10 shorter events, 0.1 us)
Async XLA Ops:
  0.6 1.6 %copy-start = (bf16[128,8192]{1,0:T(8,128)(2,1)S(1)}, bf16[128,8192]{1,0:T(8,128)(2,1)}, u32[]{:S(2)}) copy-start(bf16[128,8192]{1,0:T(8,128)(2,1)} %tokens_ref.1) | copy-start | bytes 6291460
  2.2 3.5 %copy-start.2 = (f32[8,256]{1,0:T(8,128)S(1)}, f32[8,256]{1,0:T(8,128)}, u32[]{:S(2)}) copy-start(f32[8,256]{1,0:T(8,128)} %param.12) | copy-start | bytes 24580
  2.2 3.5 %copy-start.3 = (f32[8,256]{1,0:T(8,128)S(1)}, f32[8,256]{1,0:T(8,128)}, u32[]{:S(2)}) copy-start(f32[8,256]{1,0:T(8,128)} %param.11) | copy-start | bytes 24580
  2.2 3.6 %copy-start.4 = (f32[8,256]{1,0:T(8,128)S(1)}, f32[8,256]{1,0:T(8,128)}, u32[]{:S(2)}) copy-start(f32[8,256]{1,0:T(8,128)} %param.13) | copy-start | bytes 24580
  2.2 3.6 %copy-start.5 = (f32[8,256]{1,0:T(8,128)S(1)}, f32[8,256]{1,0:T(8,128)}, u32[]{:S(2)}) copy-start(f32[8,256]{1,0:T(8,128)} %param.14) | copy-start | bytes 24580
  2.2 45.6 %copy-start.6 = (s32[128]{0:T(128)S(1)}, s32[128]{0:T(128)}, u32[]{:S(2)}) copy-start(s32[128]{0:T(128)} %param.10) | copy-start | bytes 1540
  3.1 81.2 %collective-permute-start = (bf16[4,128,2048]{2,1,0:T(8,128)(2,1)S(1)}, bf16[4,128,2048]{2,1,0:T(8,128)(2,1)}, u32[]{:S(2)}, u32[]{:S(2)}) collective-permute-start(bf16[4,128,2048]{2,1,0:T(8,128)(2,1)S(1)} %shard_map.111.mine_ref), channel_id=1, source_target_pairs={{0,1},{1,0},{2,3},{3,2},{4,5},{5,4},{6,7},{7,6},{8,9},{9,8},{10,11... | collective-permute-start | bytes 6291464 | tf_op jit(solution)/shard_map/ppermute | solution.py:294
  40.7 23.7 %all-to-all-start.1 = ((bf16[8,256,128]{2,1,0:T(8,128)(2,1)}), bf16[8,256,128]{2,1,0:T(8,128)(2,1)S(1)}, u32[]{:S(2)}, u32[]{:S(2)}) async-start(bf16[8,256,128]{2,1,0:T(8,128)(2,1)} %broadcast_in_dim.28), calls=%async_computation.1 | async-start | bytes 1048576 | tf_op jit(solution)/shard_map/all_to_all | solution.py:31
  64.4 13.7 %collective-permute-start.1 = (bf16[2048,128]{1,0:T(8,128)(2,1)S(1)}, bf16[2048,128]{1,0:T(8,128)(2,1)S(1)}, u32[]{:S(2)}, u32[]{:S(2)}) collective-permute-start(bf16[2048,128]{1,0:T(8,128)(2,1)S(1)} %bitcast.17), channel_id=1, source_target_pairs={{0,512},{2,514},{512,2},{514,0},{1,513},{3,515},{513,3},{515,1},{4... | collective-permute-start | bytes 1572872 | tf_op jit(solution)/shard_map/ppermute | solution.py:274
  66.8 15.0 %collective-permute-start.2 = (bf16[2048,128]{1,0:T(8,128)(2,1)S(1)}, bf16[2048,128]{1,0:T(8,128)(2,1)S(1)}, u32[]{:S(2)}, u32[]{:S(2)}) collective-permute-start(bf16[2048,128]{1,0:T(8,128)(2,1)S(1)} %bitcast.18), channel_id=1, source_target_pairs={{0,514},{2,512},{512,0},{514,2},{1,515},{3,513},{513,1},{515,3},{4... | collective-permute-start | bytes 1572872 | tf_op jit(solution)/shard_map/ppermute | solution.py:274
  78.2 10.5 %collective-permute-start.3 = (bf16[1024,128]{1,0:T(8,128)(2,1)S(1)}, bf16[1024,128]{1,0:T(8,128)(2,1)S(1)}, u32[]{:S(2)}, u32[]{:S(2)}) collective-permute-start(bf16[1024,128]{1,0:T(8,128)(2,1)S(1)} %slice.28), channel_id=1, source_target_pairs={{0,512},{2,514},{512,2},{514,0},{1,513},{3,515},{513,3},{515,1},{4... | collective-permute-start | bytes 786440 | tf_op jit(solution)/shard_map/ppermute | solution.py:274
  81.8 9.5 %collective-permute-start.4 = (bf16[1024,128]{1,0:T(8,128)(2,1)S(1)}, bf16[1024,128]{1,0:T(8,128)(2,1)S(1)}, u32[]{:S(2)}, u32[]{:S(2)}) collective-permute-start(bf16[1024,128]{1,0:T(8,128)(2,1)S(1)} %slice.29), channel_id=1, source_target_pairs={{0,514},{2,512},{512,0},{514,2},{1,515},{3,513},{513,1},{515,3},{4... | collective-permute-start | bytes 786440 | tf_op jit(solution)/shard_map/ppermute | solution.py:274
  93.4 23.2 %copy-start.1 = (bf16[128,1024]{1,0:T(8,128)(2,1)S(1)}, bf16[128,1024]{1,0:T(8,128)(2,1)}, u32[]{:S(2)}) copy-start(bf16[128,1024]{1,0:T(8,128)(2,1)} %queries_ref.1) | copy-start | bytes 786436
  100.0 11.1 %collective-permute-start.6 = (bf16[512,128]{1,0:T(8,128)(2,1)S(1)}, bf16[512,128]{1,0:T(8,128)(2,1)S(1)}, u32[]{:S(2)}, u32[]{:S(2)}) collective-permute-start(bf16[512,128]{1,0:T(8,128)(2,1)S(1)} %all_gather.19), channel_id=1, source_target_pairs={{0,4},{2,6},{4,8},{6,10},{8,12},{10,14},{12,16},{14,18},{16,20},{1... | collective-permute-start | bytes 393224 | tf_op jit(solution)/shard_map/ppermute | solution.py:265
  101.9 12.5 %collective-permute-start.5 = (bf16[512,128]{1,0:T(8,128)(2,1)S(1)}, bf16[512,128]{1,0:T(8,128)(2,1)S(1)}, u32[]{:S(2)}, u32[]{:S(2)}) collective-permute-start(bf16[512,128]{1,0:T(8,128)(2,1)S(1)} %all_gather.19), channel_id=1, source_target_pairs={{0,8},{2,10},{4,12},{6,14},{8,16},{10,18},{12,20},{14,22},{16,24},... | collective-permute-start | bytes 393224 | tf_op jit(solution)/shard_map/ppermute | solution.py:265

commit v4 on v3

--- a/solution.py
+++ b/solution.py
@@ -24,11 +24,6 @@
 adam_eps = 1e-08
 rope_base = 500000.0
 masked_score = -1e30
-
-
-def from_everyone(x, axis):
-    copies = jnp.broadcast_to(x, (lax.axis_size(axis), *x.shape))
-    return lax.all_to_all(copies, axis, split_axis=0, concat_axis=0, tiled=True)
 
 
 def adam_update(grad, master, moment1, moment2, step):
@@ -302,7 +297,7 @@
     first = jnp.broadcast_to(
         (jnp.arange(local_count, dtype=jnp.int32) - positions)[None, :], (8, local_count)
     )
-    over_y = from_everyone(over_z, ALONG_Y).reshape(-1, head_dim)
+    over_y = lax.all_gather(over_z, ALONG_Y, axis=0, tiled=True)
     half = over_y.shape[0] // 2
     tiles = (2 * local_count, head_dim)
     left = along_x(over_y, 1)

time: 121 us -> 127 us (1.050)
  starting transfers between devices: 25 us -> 40 us
  blocking collectives: 46 us -> 39.5 us
  waiting for transfers between devices: 32.6 us -> 29.9 us
    all_to_all x1 -> x0, blocking collectives: 33.4 us -> none  [column_halves(): return lax.all_to_all(copies, axes, split_axis=0, concat_axis=0, tiled=True)]
    all_gather x0 -> x1, blocking collectives: none -> 26.9 us  [compute(): over_y = lax.all_gather(over_z, ALONG_Y, axis=0, tiled=True)]
    all_to_all x1, starting transfers between devices: 7.1 us -> 19.3 us  [column_halves(): return lax.all_to_all(copies, axes, split_axis=0, concat_axis=0, tiled=True)]
    ppermute x2, starting transfers between devices: 4.29 us -> 7.39 us  [shifted(): lax.ppermute(value, axis, [(source, source + steps) for source in range(c...]
    all_to_all x1, waiting for transfers between devices: 14.8 us -> 12.5 us  [column_halves(): return lax.all_to_all(copies, axes, split_axis=0, concat_axis=0, tiled=True)]
  transfers between devices with their start and end apart: 8 -> 8, of which waited for: 5 -> 6; matrix products, arithmetic and copies ran while one was open for 2% -> 2% of each run, Pallas kernels for 4% -> 3%
where the time goes in v4:
time: 127 us; the launch traced here: 126 us
  starting transfers between devices  40 us (31%)
  blocking collectives  39.5 us (31%)
  waiting for transfers between devices  29.9 us (24%)
  Pallas kernels  11 us (9%)
  local copies, waits for them, and re-layouts  2.29 us (2%)
  between operations  1.61 us (1%)
  other arithmetic  1.52 us (1%)
    all_gather x1, blocking collectives, compute(): over_y = lax.all_gather(over_z, ALONG_Y, axis=0, tiled=True)  26.9 us
    all_to_all x1, starting transfers between devices, column_halves(): return lax.all_to_all(copies, axes, split_axis=0, concat_axis=0, tiled=True)  19.3 us
    all_to_all x1, waiting for transfers between devices, column_halves(): return lax.all_to_all(copies, axes, split_axis=0, concat_axis=0, tiled=True)  12.5 us
    ppermute x4, starting transfers between devices, along_x(): return lax.ppermute(value, ALONG_X, pairs)  11.5 us
    ppermute x4, waiting for transfers between devices, along_x(): return lax.ppermute(value, ALONG_X, pairs)  10.1 us
    ppermute x2, starting transfers between devices, shifted(): lax.ppermute(value, axis, [(source, source + steps) for source in range(c...  7.39 us
    ppermute x2, waiting for transfers between devices, shifted(): lax.ppermute(value, axis, [(source, source + steps) for source in range(c...  7.26 us
    all_gather x1, blocking collectives, compute(): row_kv = lax.all_gather(half_kv, X_HI, axis=0, tiled=True)  6.57 us
  transfers between devices with their start and end apart: 8, of which 6 were waited for; matrix products, arithmetic and copies ran while one was open for 2% of the time, Pallas kernels for 3%

profile of v4, /device:TPU:6, one launch (start us, length us, event | category | flops | bytes accessed | tf_op | source)
XLA Modules:
  0.0 125.9 jit_solution(10913269372368213338)
XLA Ops:
  0.6 0.0 copy-start
  0.6 1.6 %copy-done = bf16[128,8192]{1,0:T(8,128)(2,1)S(1)} copy-done((bf16[128,8192]{1,0:T(8,128)(2,1)S(1)}, bf16[128,8192]{1,0:T(8,128)(2,1)}, u32[]{:S(2)}) %copy-start) | copy-done | bytes 2097176
  2.2 0.0 copy-start.2
  2.2 0.0 copy-start.3
  2.2 0.0 copy-start.4
  2.2 0.0 copy-start.5
  2.2 0.0 copy-start.6
  2.2 0.8 shard_map.111.mine_ref
  3.1 1.9 %collective-permute-start = (bf16[4,128,2048]{2,1,0:T(8,128)(2,1)S(1)}, bf16[4,128,2048]{2,1,0:T(8,128)(2,1)}, u32[]{:S(2)}, u32[]{:S(2)}) collective-permute-start(bf16[4,128,2048]{2,1,0:T(8,128)(2,1)S(1)} %shard_map.111.mine_ref), channel_id=1, source_target_pairs={{0,1},{1,0},{2,3},{3,2},{4,5},{5,4},{6,7},{7,6},{8,9},{9,8},{10,11... | collective-permute-start | bytes 6291464 | tf_op jit(solution)/shard_map/ppermute | solution.py:289
  5.8 0.0 copy-done.2
  5.8 0.0 copy-done.3
  5.8 0.0 copy-done.4
  5.8 0.0 copy-done.5
  5.8 0.6 fusion.5
  6.4 0.6 broadcast_in_dim.24
  7.1 19.3 %all-to-all-start = ((bf16[32,8,128]{2,1,0:T(8,128)(2,1)}), bf16[32,8,128]{2,1,0:T(8,128)(2,1)S(1)}, u32[]{:S(2)}, u32[]{:S(2)}) async-start(bf16[32,8,128]{2,1,0:T(8,128)(2,1)} %bitcast.7), calls=%async_computation | async-start | bytes 131072 | tf_op jit(solution)/shard_map/all_to_all | solution.py:277
  26.4 0.0 copy-done.6
  26.4 1.8 %all-gather.2 = s32[2,1,128]{2,1,0:T(1,128)S(1)} all-gather(s32[1,1,128]{2,1,0:T(1,128)S(1)} %bitcast.19), channel_id=1, replica_groups=mesh['x_lo'=2,'z'=16,'y'=8,'x_hi'=2,'core'=2] {'core'}, dimensions={0}, use_global_device_ids=true | all-gather | bytes 1536 | tf_op jit(solution)/shard_map/all_gather | solution.py:290
  28.2 12.5 %all-to-all-done = bf16[32,8,128]{2,1,0:T(8,128)(2,1)S(1)} async-done(((bf16[32,8,128]{2,1,0:T(8,128)(2,1)}), bf16[32,8,128]{2,1,0:T(8,128)(2,1)S(1)}, u32[]{:S(2)}, u32[]{:S(2)}) %all-to-all-start) | async-done | bytes 65568 | tf_op jit(solution)/shard_map/all_to_all | solution.py:277
  40.7 26.9 %all_gather.21.piece_ref = bf16[2048,128]{1,0:T(8,128)(2,1)S(1)} all-gather(bf16[256,128]{1,0:T(8,128)(2,1)S(1)} %bitcast.18), channel_id=1, replica_groups=mesh['x_lo'=2,'z'=16,'y'=8,'x_hi'=2,'core'=2] {'y'}, dimensions={0}, use_global_device_ids=true | all-gather | bytes 589824 | tf_op jit(solution)/shard_map/all_gather | solution.py:300
  67.6 2.4 %collective-permute-start.1 = (bf16[2048,128]{1,0:T(8,128)(2,1)S(1)}, bf16[2048,128]{1,0:T(8,128)(2,1)S(1)}, u32[]{:S(2)}, u32[]{:S(2)}) collective-permute-start(bf16[2048,128]{1,0:T(8,128)(2,1)S(1)} %all_gather.21.piece_ref), channel_id=1, source_target_pairs={{0,512},{2,514},{512,2},{514,0},{1,513},{3,515},{513,3},{515,1},{4... | collective-permute-start | bytes 1572872 | tf_op jit(solution)/shard_map/ppermute | solution.py:269
  70.0 3.5 %collective-permute-start.2 = (bf16[2048,128]{1,0:T(8,128)(2,1)S(1)}, bf16[2048,128]{1,0:T(8,128)(2,1)S(1)}, u32[]{:S(2)}, u32[]{:S(2)}) collective-permute-start(bf16[2048,128]{1,0:T(8,128)(2,1)S(1)} %all_gather.21.piece_ref), channel_id=1, source_target_pairs={{0,514},{2,512},{512,0},{514,2},{1,515},{3,513},{513,1},{515,3},{4... | collective-permute-start | bytes 1572872 | tf_op jit(solution)/shard_map/ppermute | solution.py:269
  73.5 0.5 fusion
  74.0 7.5 %collective-permute-done.1.left_ref = bf16[2048,128]{1,0:T(8,128)(2,1)S(1)} collective-permute-done((bf16[2048,128]{1,0:T(8,128)(2,1)S(1)}, bf16[2048,128]{1,0:T(8,128)(2,1)S(1)}, u32[]{:S(2)}, u32[]{:S(2)}) %collective-permute-start.1) | collective-permute-done | bytes 524320 | tf_op jit(solution)/shard_map/ppermute | solution.py:269
  81.5 2.6 %collective-permute-start.3 = (bf16[1024,128]{1,0:T(8,128)(2,1)S(1)}, bf16[1024,128]{1,0:T(8,128)(2,1)S(1)}, u32[]{:S(2)}, u32[]{:S(2)}) collective-permute-start(bf16[1024,128]{1,0:T(8,128)(2,1)S(1)} %slice.28), channel_id=1, source_target_pairs={{0,512},{2,514},{512,2},{514,0},{1,513},{3,515},{513,3},{515,1},{4... | collective-permute-start | bytes 786440 | tf_op jit(solution)/shard_map/ppermute | solution.py:269
  84.1 0.2 collective-permute-done.2.right_ref
  84.4 3.1 %collective-permute-start.4 = (bf16[1024,128]{1,0:T(8,128)(2,1)S(1)}, bf16[1024,128]{1,0:T(8,128)(2,1)S(1)}, u32[]{:S(2)}, u32[]{:S(2)}) collective-permute-start(bf16[1024,128]{1,0:T(8,128)(2,1)S(1)} %slice.29), channel_id=1, source_target_pairs={{0,514},{2,512},{512,0},{514,2},{1,515},{3,513},{513,1},{515,3},{4... | collective-permute-start | bytes 786440 | tf_op jit(solution)/shard_map/ppermute | solution.py:269
  87.4 0.1 pad_add_fusion.place_ref
  87.5 0.1 maximum_select_fusion
  87.6 0.0 collective-permute-done.theirs_ref
  87.7 2.1 %shard_map.112.so_far_ref = f32[256,128]{1,0:T(8,128)S(1)} custom-call(s32[2]{0:T(128)S(1)} %pad_add_fusion.place_ref, bf16[4,128,2048]{2,1,0:T(8,128)(2,1)} %collective-permute-done.theirs_ref, bf16[4,128,2048]{2,1,0:T(8,128)(2,1)S(1)} %shard_map.111.mine_ref, bf16[2048,128]{1,0:T(8,128)(2,1)S(1)} %all_gather.21.piece_ref), custom_call_target="tpu_custom_call" | custom-call | flops 134217728 | bytes 1572864 | tf_op jit(solution)/shard_map/pallas_call | solution.py:144
  89.7 2.3 %shard_map.113.so_far_ref = f32[256,128]{1,0:T(8,128)S(1)} custom-call(s32[2]{0:T(128)S(1)} %pad_add_fusion.place_ref, bf16[4,128,2048]{2,1,0:T(8,128)(2,1)} %collective-permute-done.theirs_ref, bf16[4,128,2048]{2,1,0:T(8,128)(2,1)S(1)} %shard_map.111.mine_ref, f32[256,128]{1,0:T(8,128)S(1)} %shard_map.112.so_far_ref, ...), custom_call_target="tpu_custom_call" | custom-call | flops 268435456 | bytes 3145728 | tf_op jit(solution)/shard_map/pallas_call | solution.py:144
  92.1 0.0 collective-permute-done.3.low_ref
  92.1 2.5 %collective-permute-done.4.high_ref = bf16[1024,128]{1,0:T(8,128)(2,1)S(1)} collective-permute-done((bf16[1024,128]{1,0:T(8,128)(2,1)S(1)}, bf16[1024,128]{1,0:T(8,128)(2,1)S(1)}, u32[]{:S(2)}, u32[]{:S(2)}) %collective-permute-start.4) | collective-permute-done | bytes 262176 | tf_op jit(solution)/shard_map/ppermute | solution.py:269
  94.5 2.1 %shard_map.114 = bf16[256,128]{1,0:T(8,128)(2,1)S(1)} custom-call(s32[2]{0:T(128)S(1)} %pad_add_fusion.place_ref, bf16[4,128,2048]{2,1,0:T(8,128)(2,1)} %collective-permute-done.theirs_ref, bf16[4,128,2048]{2,1,0:T(8,128)(2,1)S(1)} %shard_map.111.mine_ref, f32[256,128]{1,0:T(8,128)S(1)} %shard_map.113.so_far_ref, ...), custom_call_target="tpu_custom_call" | custom-call | flops 134217728 | bytes 1572864 | tf_op jit(solution)/shard_map/pallas_call | solution.py:144
  96.7 0.0 copy-start.1
  96.7 6.6 %all_gather.23 = bf16[512,128]{1,0:T(8,128)(2,1)S(1)} all-gather(bf16[256,128]{1,0:T(8,128)(2,1)S(1)} %shard_map.114), channel_id=1, replica_groups=mesh['x_lo'=2,'z'=16,'y'=8,'x_hi'=2,'core'=2] {'x_hi'}, dimensions={0}, use_global_device_ids=true | all-gather | bytes 196608 | tf_op jit(solution)/shard_map/all_gather | solution.py:313
  103.3 3.4 %collective-permute-start.6 = (bf16[512,128]{1,0:T(8,128)(2,1)S(1)}, bf16[512,128]{1,0:T(8,128)(2,1)S(1)}, u32[]{:S(2)}, u32[]{:S(2)}) collective-permute-start(bf16[512,128]{1,0:T(8,128)(2,1)S(1)} %all_gather.23), channel_id=1, source_target_pairs={{0,4},{2,6},{4,8},{6,10},{8,12},{10,14},{12,16},{14,18},{16,20},{1... | collective-permute-start | bytes 393224 | tf_op jit(solution)/shard_map/ppermute | solution.py:260
  106.7 4.0 %collective-permute-start.5 = (bf16[512,128]{1,0:T(8,128)(2,1)S(1)}, bf16[512,128]{1,0:T(8,128)(2,1)S(1)}, u32[]{:S(2)}, u32[]{:S(2)}) collective-permute-start(bf16[512,128]{1,0:T(8,128)(2,1)S(1)} %all_gather.23), channel_id=1, source_target_pairs={{0,8},{2,10},{4,12},{6,14},{8,16},{10,18},{12,20},{14,22},{16,24},... | collective-permute-start | bytes 393224 | tf_op jit(solution)/shard_map/ppermute | solution.py:260
  110.7 0.1 pad_maximum_fusion.1
  110.8 2.0 %all-gather.1 = bf16[1024,128]{1,0:T(8,128)(2,1)S(1)} all-gather(bf16[512,128]{1,0:T(8,128)(2,1)S(1)} %all_gather.23), channel_id=3, replica_groups=mesh['x_lo'=2,'z'=16,'y'=8,'x_hi'=2,'core'=2] {'core'}, dimensions={0}, use_global_device_ids=true | all-gather | bytes 393216 | tf_op jit(solution)/shard_map/all_gather | solution.py:316
  112.8 1.6 %collective-permute-done.6 = bf16[512,128]{1,0:T(8,128)(2,1)S(1)} collective-permute-done((bf16[512,128]{1,0:T(8,128)(2,1)S(1)}, bf16[512,128]{1,0:T(8,128)(2,1)S(1)}, u32[]{:S(2)}, u32[]{:S(2)}) %collective-permute-start.6) | collective-permute-done | bytes 131104 | tf_op jit(solution)/shard_map/ppermute | solution.py:260
  114.3 5.7 %collective-permute-done.5 = bf16[512,128]{1,0:T(8,128)(2,1)S(1)} collective-permute-done((bf16[512,128]{1,0:T(8,128)(2,1)S(1)}, bf16[512,128]{1,0:T(8,128)(2,1)S(1)}, u32[]{:S(2)}, u32[]{:S(2)}) %collective-permute-start.5) | collective-permute-done | bytes 131104 | tf_op jit(solution)/shard_map/ppermute | solution.py:260
  120.1 2.2 %all-gather = bf16[2048,128]{1,0:T(8,128)(2,1)S(1)} all-gather(bf16[1024,128]{1,0:T(8,128)(2,1)S(1)} %pad_maximum_fusion), channel_id=2, replica_groups=mesh['x_lo'=2,'z'=16,'y'=8,'x_hi'=2,'core'=2] {'core'}, dimensions={0}, use_global_device_ids=true | all-gather | bytes 786432 | tf_op jit(solution)/shard_map/all_gather | solution.py:317
  122.2 0.0 copy-done.1
  122.3 3.6 %shard_map.115 = bf16[128,1024]{1,0:T(8,128)(2,1)} custom-call(s32[1]{0:T(128)} %bitcast.offset_ref, bf16[2,1024,128]{2,1,0:T(8,128)(2,1)S(1)} %bitcast.16, bf16[2,512,128]{2,1,0:T(8,128)(2,1)S(1)} %bitcast.17, bf16[128,1024]{1,0:T(8,128)(2,1)S(1)} %copy-done.1, s32[8,128]{1,0:T(8,128)S(1)} %broadcast_in_dim.27.first_ref, ...), custom_call_target="tpu_custom_call" | custom-call | flops 905969664 | bytes 1310720 | tf_op jit(solution)/shard_map/pallas_call | solution.py:229
  (9 shorter events, 0.1 us)
Async XLA Ops:
  0.6 1.6 %copy-start = (bf16[128,8192]{1,0:T(8,128)(2,1)S(1)}, bf16[128,8192]{1,0:T(8,128)(2,1)}, u32[]{:S(2)}) copy-start(bf16[128,8192]{1,0:T(8,128)(2,1)} %tokens_ref.1) | copy-start | bytes 6291460
  2.2 3.5 %copy-start.2 = (f32[8,256]{1,0:T(8,128)S(1)}, f32[8,256]{1,0:T(8,128)}, u32[]{:S(2)}) copy-start(f32[8,256]{1,0:T(8,128)} %param.12) | copy-start | bytes 24580
  2.2 3.5 %copy-start.3 = (f32[8,256]{1,0:T(8,128)S(1)}, f32[8,256]{1,0:T(8,128)}, u32[]{:S(2)}) copy-start(f32[8,256]{1,0:T(8,128)} %param.11) | copy-start | bytes 24580
  2.2 3.6 %copy-start.4 = (f32[8,256]{1,0:T(8,128)S(1)}, f32[8,256]{1,0:T(8,128)}, u32[]{:S(2)}) copy-start(f32[8,256]{1,0:T(8,128)} %param.13) | copy-start | bytes 24580
  2.2 3.6 %copy-start.5 = (f32[8,256]{1,0:T(8,128)S(1)}, f32[8,256]{1,0:T(8,128)}, u32[]{:S(2)}) copy-start(f32[8,256]{1,0:T(8,128)} %param.14) | copy-start | bytes 24580
  2.2 24.1 %copy-start.6 = (s32[128]{0:T(128)S(1)}, s32[128]{0:T(128)}, u32[]{:S(2)}) copy-start(s32[128]{0:T(128)} %param.10) | copy-start | bytes 1540
  3.1 84.5 %collective-permute-start = (bf16[4,128,2048]{2,1,0:T(8,128)(2,1)S(1)}, bf16[4,128,2048]{2,1,0:T(8,128)(2,1)}, u32[]{:S(2)}, u32[]{:S(2)}) collective-permute-start(bf16[4,128,2048]{2,1,0:T(8,128)(2,1)S(1)} %shard_map.111.mine_ref), channel_id=1, source_target_pairs={{0,1},{1,0},{2,3},{3,2},{4,5},{5,4},{6,7},{7,6},{8,9},{9,8},{10,11... | collective-permute-start | bytes 6291464 | tf_op jit(solution)/shard_map/ppermute | solution.py:289
  7.1 33.6 %all-to-all-start = ((bf16[32,8,128]{2,1,0:T(8,128)(2,1)}), bf16[32,8,128]{2,1,0:T(8,128)(2,1)S(1)}, u32[]{:S(2)}, u32[]{:S(2)}) async-start(bf16[32,8,128]{2,1,0:T(8,128)(2,1)} %bitcast.7), calls=%async_computation | async-start | bytes 131072 | tf_op jit(solution)/shard_map/all_to_all | solution.py:277
  67.6 13.9 %collective-permute-start.1 = (bf16[2048,128]{1,0:T(8,128)(2,1)S(1)}, bf16[2048,128]{1,0:T(8,128)(2,1)S(1)}, u32[]{:S(2)}, u32[]{:S(2)}) collective-permute-start(bf16[2048,128]{1,0:T(8,128)(2,1)S(1)} %all_gather.21.piece_ref), channel_id=1, source_target_pairs={{0,512},{2,514},{512,2},{514,0},{1,513},{3,515},{513,3},{515,1},{4... | collective-permute-start | bytes 1572872 | tf_op jit(solution)/shard_map/ppermute | solution.py:269
  70.0 14.3 %collective-permute-start.2 = (bf16[2048,128]{1,0:T(8,128)(2,1)S(1)}, bf16[2048,128]{1,0:T(8,128)(2,1)S(1)}, u32[]{:S(2)}, u32[]{:S(2)}) collective-permute-start(bf16[2048,128]{1,0:T(8,128)(2,1)S(1)} %all_gather.21.piece_ref), channel_id=1, source_target_pairs={{0,514},{2,512},{512,0},{514,2},{1,515},{3,513},{513,1},{515,3},{4... | collective-permute-start | bytes 1572872 | tf_op jit(solution)/shard_map/ppermute | solution.py:269
  81.5 10.5 %collective-permute-start.3 = (bf16[1024,128]{1,0:T(8,128)(2,1)S(1)}, bf16[1024,128]{1,0:T(8,128)(2,1)S(1)}, u32[]{:S(2)}, u32[]{:S(2)}) collective-permute-start(bf16[1024,128]{1,0:T(8,128)(2,1)S(1)} %slice.28), channel_id=1, source_target_pairs={{0,512},{2,514},{512,2},{514,0},{1,513},{3,515},{513,3},{515,1},{4... | collective-permute-start | bytes 786440 | tf_op jit(solution)/shard_map/ppermute | solution.py:269
  84.4 10.2 %collective-permute-start.4 = (bf16[1024,128]{1,0:T(8,128)(2,1)S(1)}, bf16[1024,128]{1,0:T(8,128)(2,1)S(1)}, u32[]{:S(2)}, u32[]{:S(2)}) collective-permute-start(bf16[1024,128]{1,0:T(8,128)(2,1)S(1)} %slice.29), channel_id=1, source_target_pairs={{0,514},{2,512},{512,0},{514,2},{1,515},{3,513},{513,1},{515,3},{4... | collective-permute-start | bytes 786440 | tf_op jit(solution)/shard_map/ppermute | solution.py:269
  96.7 25.6 %copy-start.1 = (bf16[128,1024]{1,0:T(8,128)(2,1)S(1)}, bf16[128,1024]{1,0:T(8,128)(2,1)}, u32[]{:S(2)}) copy-start(bf16[128,1024]{1,0:T(8,128)(2,1)} %queries_ref.1) | copy-start | bytes 786436
  103.3 11.1 %collective-permute-start.6 = (bf16[512,128]{1,0:T(8,128)(2,1)S(1)}, bf16[512,128]{1,0:T(8,128)(2,1)S(1)}, u32[]{:S(2)}, u32[]{:S(2)}) collective-permute-start(bf16[512,128]{1,0:T(8,128)(2,1)S(1)} %all_gather.23), channel_id=1, source_target_pairs={{0,4},{2,6},{4,8},{6,10},{8,12},{10,14},{12,16},{14,18},{16,20},{1... | collective-permute-start | bytes 393224 | tf_op jit(solution)/shard_map/ppermute | solution.py:260
  106.7 13.4 %collective-permute-start.5 = (bf16[512,128]{1,0:T(8,128)(2,1)S(1)}, bf16[512,128]{1,0:T(8,128)(2,1)S(1)}, u32[]{:S(2)}, u32[]{:S(2)}) collective-permute-start(bf16[512,128]{1,0:T(8,128)(2,1)S(1)} %all_gather.23), channel_id=1, source_target_pairs={{0,8},{2,10},{4,12},{6,14},{8,16},{10,18},{12,20},{14,22},{16,24},... | collective-permute-start | bytes 393224 | tf_op jit(solution)/shard_map/ppermute | solution.py:260
